TPU v7x, 512 devices: a whole 4x8x8 slice. The times are simulated.
512 devices in a mesh: axial: 32 (over x, z), azim: 8 (over y), bank: 2 (over core).
Axes of the slice: x: 4, y: 8, z: 8, core: 2. Of those that a mesh axis runs over, the one named last changes fastest.
Arguments:
- adjoint_state: float32 [2, 64, 256, 2048], P('bank', None, 'axial', 'azim'), may hold values from -6 to 6
- adjoint_source: float32 [2, 64, 256, 2048], P('bank', None, 'axial', 'azim'), may hold values from -6 to 6
- reaction_rate: float32 [2, 256, 2048], P('bank', 'axial', 'azim'), may hold values from 0.5 to 2
- jacobian: float32 [2, 64, 64], P('bank'), may hold values from -0.75 to 0.75
- lifting: float32 [2, 6, 256, 2048], P('bank', None, 'axial', 'azim'), may hold values from -0.125 to 0.125
- separator: int32 [32, 8, 2, 6], P('axial', 'azim', 'bank'), may hold values from 0 to 2047
- leaf_schur: float32 [32, 8, 2, 384, 384], P('axial', 'azim', 'bank'), may hold values from -14 to 43, as said below
Outputs:
- interface_adjoint: float32 [32, 8, 2, 384], P('axial', 'azim', 'bank')
Inputs may be any that keep to these rules, and one draw needn't show every extreme that they name: `separator`: a cell k = row * 256 + column of the device's own block. `leaf_schur`: every leaf block is symmetric positive definite.
All inputs are finite; a program needn't handle non-finite values.
Results may differ from a plain program's by a relative error of at most 0.0003.
Values sent between devices are 32-bit elements; how exact they have to be, the bound alone decides.
A program may use at most 64 MiB of HBM per device.

v0:
```python
import jax
import jax.numpy as jnp
from jax import lax
from jax.sharding import PartitionSpec as P

highest = lax.Precision.HIGHEST
diffusion = 0.5


def extended(array, sides, width, wrap):
    for axis, dim in sides:
        size, length = (lax.axis_size(axis), array.shape[dim])
        up = [(i, (i + 1) % size) for i in range(size if wrap else size - 1)]
        down = [(j, i) for i, j in up]
        last = lax.slice_in_dim(array, length - width, length, axis=dim)
        first = lax.slice_in_dim(array, 0, width, axis=dim)
        before = lax.ppermute(last, axis, up)
        after = lax.ppermute(first, axis, down)
        array = jnp.concatenate([before, array, after], axis=dim)
    return array


def partner(array, axis, distance):
    return lax.ppermute(array, axis, [(i, i ^ 1 << distance) for i in range(lax.axis_size(axis))])


def eliminate(first_shared, second_shared, shared_rhs, middle):
    shared_sum = first_shared[:, middle:] + second_shared[:, middle:]
    factor = jnp.linalg.cholesky(shared_sum)
    coupling = jnp.concatenate([first_shared[:, :middle], second_shared[:, :middle]], axis=1)
    inner = jax.scipy.linalg.solve_triangular(factor, coupling, lower=True)
    coupled = jax.scipy.linalg.solve_triangular(factor, inner, lower=True, trans=1)
    inner_rhs = jax.scipy.linalg.solve_triangular(factor, shared_rhs, lower=True)
    shifted = jax.scipy.linalg.solve_triangular(factor, inner_rhs, lower=True, trans=1)
    return (coupled, shifted)


def body(adjoint_state, adjoint_source, reaction_rate, jacobian, lifting, separator, leaf_schur):
    along_axial = extended(adjoint_state, (("axial", 2),), 1, False)
    along_azim = extended(adjoint_state, (("azim", 3),), 1, True)
    scaled = reaction_rate[:, None] * adjoint_state
    reaction = jnp.einsum("bvu,bvxz->buxz", jacobian, scaled, precision=highest)
    neighbours = along_axial[:, :, 2:, :] + along_axial[:, :, :-2, :]
    neighbours = neighbours + along_azim[:, :, :, :-2] + along_azim[:, :, :, 2:]
    residual = adjoint_source - reaction - diffusion * (4.0 * adjoint_state - neighbours)
    chans = residual.shape[1]
    flat_residual = residual.reshape(chans, -1)
    sep_cells = separator.reshape(-1)
    picked = jnp.take(flat_residual, sep_cells, axis=1).T
    lifted = jnp.einsum(
        "ck,vk->cv", lifting.reshape(sep_cells.shape[0], -1), flat_residual, precision=highest
    )
    rhs = (picked + lifted).reshape(-1)
    width = rhs.shape[0]
    middle = width // 2
    schur = leaf_schur.reshape(width, width)
    levels = lax.axis_size(("axial", "azim", "bank")).bit_length() - 1
    flat_index = lax.axis_index(("axial", "azim", "bank"))
    saved_levels = []
    for level in range(levels):
        is_lower = jnp.equal(jnp.bitwise_and(jnp.right_shift(flat_index, level), 1), 0)
        other_schur, other_rhs = partner((schur, rhs), ("axial", "azim", "bank"), level)
        first_shared = jnp.where(is_lower, schur[middle:], other_schur[middle:])
        second_shared = jnp.where(is_lower, other_schur[middle:], schur[middle:])
        coupled, shifted = eliminate(
            first_shared, second_shared, rhs[middle:] + other_rhs[middle:], middle
        )
        first_cross = jnp.where(is_lower, schur[:middle, middle:], other_schur[:middle, middle:])
        second_cross = jnp.where(is_lower, other_schur[:middle, middle:], schur[:middle, middle:])
        first_outer = jnp.where(is_lower, schur[:middle, :middle], other_schur[:middle, :middle])
        second_outer = jnp.where(is_lower, other_schur[:middle, :middle], schur[:middle, :middle])
        outer_rhs = jnp.where(
            is_lower,
            jnp.concatenate([rhs[:middle], other_rhs[:middle]]),
            jnp.concatenate([other_rhs[:middle], rhs[:middle]]),
        )
        stacked_cross = jnp.concatenate([first_cross, second_cross], axis=0)
        parent = -jnp.dot(stacked_cross, coupled, precision=highest)
        parent = parent.at[:middle, :middle].add(first_outer)
        parent = parent.at[middle:, middle:].add(second_outer)
        schur = parent
        rhs = outer_rhs - jnp.dot(stacked_cross, shifted, precision=highest)
        saved_levels.append((coupled, shifted, is_lower))
    root_factor = jnp.linalg.cholesky(schur)
    inner = jax.scipy.linalg.solve_triangular(root_factor, rhs, lower=True)
    answer = jax.scipy.linalg.solve_triangular(root_factor, inner, lower=True, trans=1)
    for coupled, shifted, is_lower in reversed(saved_levels):
        separator_values = shifted - jnp.dot(coupled, answer, precision=highest)
        outer_values = jnp.where(is_lower, answer[:middle], answer[middle:])
        answer = jnp.concatenate([outer_values, separator_values])
    return answer.reshape(1, 1, 1, width)


def solution(mesh):
    in_specs = (
        P("bank", None, "axial", "azim"),
        P("bank", None, "axial", "azim"),
        P("bank", "axial", "azim"),
        P("bank", None, None),
        P("bank", None, "axial", "azim"),
        P("axial", "azim", "bank", None),
        P("axial", "azim", "bank", None, None),
    )
    out_specs = P("axial", "azim", "bank", None)
    return jax.shard_map(body, mesh=mesh, in_specs=in_specs, out_specs=out_specs, check_vma=False)
```

profile of v0, /device:TPU:1, one launch (start us, length us, event | category | flops | bytes accessed | tf_op | source)
XLA Modules:
  0.0 903.5 jit_solution(619901082187702063)
XLA Ops:
  1.4 8.8 collective-permute-start
  13.0 3.4 collective-permute-start.11
  32.0 11.7 %cholesky.650 = f32[128,128]{1,0:T(8,128)S(1)} custom-call(f32[128,128]{1,0:T(8,128)S(1)} %cholesky.988), custom_call_target="Cholesky" | custom-call | tf_op jit(solution)/shard_map/jit(cholesky)/cholesky | solution.py:29
  43.7 9.8 %custom-call.89 = f32[1,128,128]{1,2,0:T(8,128)S(1)} custom-call(f32[1,128,128]{2,1,0:T(8,128)S(1)} %get-tuple-element.619), custom_call_target="InvertDiagBlocksLowerTriangular" | custom-call | tf_op jit(solution)/shard_map/jit(cholesky)/cholesky | solution.py:29
  53.9 5.8 cholesky.670
  62.6 20.1 %custom-call.91 = f32[2,128,128]{1,2,0:T(8,128)S(1)} custom-call(f32[2,128,128]{2,1,0:T(8,128)S(1)} %pad_maximum_fusion.67), custom_call_target="InvertDiagBlocksLowerTriangular" | custom-call | tf_op jit(solution)/shard_map/jit(_solve_triangular)/triangular_solve | solution.py:32
  99.1 9.8 %collective-permute-done.14 = f32[384]{0:T(512)S(1)} collective-permute-done((f32[384]{0:T(512)S(1)}, f32[384]{0:T(512)S(1)}, u32[]{:S(2)}, u32[]{:S(2)}) %collective-permute-start.14) | collective-permute-done | bytes 1568 | tf_op jit(solution)/shard_map/ppermute | solution.py:24
  110.1 11.7 %cholesky.688 = f32[128,128]{1,0:T(8,128)S(1)} custom-call(f32[128,128]{1,0:T(8,128)S(1)} %cholesky.991), custom_call_target="Cholesky" | custom-call | tf_op jit(solution)/shard_map/jit(cholesky)/cholesky | solution.py:29
  121.9 9.8 %custom-call.92 = f32[1,128,128]{1,2,0:T(8,128)S(1)} custom-call(f32[1,128,128]{2,1,0:T(8,128)S(1)} %get-tuple-element.617), custom_call_target="InvertDiagBlocksLowerTriangular" | custom-call | tf_op jit(solution)/shard_map/jit(cholesky)/cholesky | solution.py:29
  132.1 5.8 cholesky.708
  140.7 19.9 %custom-call.94 = f32[2,128,128]{1,2,0:T(8,128)S(1)} custom-call(f32[2,128,128]{2,1,0:T(8,128)S(1)} %pad_maximum_fusion.68), custom_call_target="InvertDiagBlocksLowerTriangular" | custom-call | tf_op jit(solution)/shard_map/jit(_solve_triangular)/triangular_solve | solution.py:32
  174.7 3.4 collective-permute-start.15
  178.7 21.5 %collective-permute-done.15 = f32[384]{0:T(512)S(1)} collective-permute-done((f32[384]{0:T(512)S(1)}, f32[384]{0:T(512)S(1)}, u32[]{:S(2)}, u32[]{:S(2)}) %collective-permute-start.15) | collective-permute-done | bytes 1568 | tf_op jit(solution)/shard_map/ppermute | solution.py:24
  200.8 11.7 %cholesky.726 = f32[128,128]{1,0:T(8,128)S(1)} custom-call(f32[128,128]{1,0:T(8,128)S(1)} %cholesky.994), custom_call_target="Cholesky" | custom-call | tf_op jit(solution)/shard_map/jit(cholesky)/cholesky | solution.py:29
  212.6 9.8 %custom-call.95 = f32[1,128,128]{1,2,0:T(8,128)S(1)} custom-call(f32[1,128,128]{2,1,0:T(8,128)S(1)} %get-tuple-element.615), custom_call_target="InvertDiagBlocksLowerTriangular" | custom-call | tf_op jit(solution)/shard_map/jit(cholesky)/cholesky | solution.py:29
  222.7 5.8 cholesky.746
  231.5 20.1 %custom-call.97 = f32[2,128,128]{1,2,0:T(8,128)S(1)} custom-call(f32[2,128,128]{2,1,0:T(8,128)S(1)} %pad_maximum_fusion.69), custom_call_target="InvertDiagBlocksLowerTriangular" | custom-call | tf_op jit(solution)/shard_map/jit(_solve_triangular)/triangular_solve | solution.py:32
  260.5 4.8 collective-permute-start.3
  268.4 4.5 collective-permute-start.16
  273.5 20.6 %collective-permute-done.16 = f32[384]{0:T(512)S(1)} collective-permute-done((f32[384]{0:T(512)S(1)}, f32[384]{0:T(512)S(1)}, u32[]{:S(2)}, u32[]{:S(2)}) %collective-permute-start.16) | collective-permute-done | bytes 1568 | tf_op jit(solution)/shard_map/ppermute | solution.py:24
  295.3 11.7 %cholesky.764 = f32[128,128]{1,0:T(8,128)S(1)} custom-call(f32[128,128]{1,0:T(8,128)S(1)} %cholesky.997), custom_call_target="Cholesky" | custom-call | tf_op jit(solution)/shard_map/jit(cholesky)/cholesky | solution.py:29
  307.1 9.8 %custom-call.98 = f32[1,128,128]{1,2,0:T(8,128)S(1)} custom-call(f32[1,128,128]{2,1,0:T(8,128)S(1)} %get-tuple-element.613), custom_call_target="InvertDiagBlocksLowerTriangular" | custom-call | tf_op jit(solution)/shard_map/jit(cholesky)/cholesky | solution.py:29
  317.3 5.8 cholesky.784
  325.9 19.9 %custom-call.100 = f32[2,128,128]{1,2,0:T(8,128)S(1)} custom-call(f32[2,128,128]{2,1,0:T(8,128)S(1)} %pad_maximum_fusion.70), custom_call_target="InvertDiagBlocksLowerTriangular" | custom-call | tf_op jit(solution)/shard_map/jit(_solve_triangular)/triangular_solve | solution.py:32
  360.3 3.6 collective-permute-start.17
  364.5 6.6 collective-permute-done.17
  372.2 11.7 %cholesky.802 = f32[128,128]{1,0:T(8,128)S(1)} custom-call(f32[128,128]{1,0:T(8,128)S(1)} %cholesky.1000), custom_call_target="Cholesky" | custom-call | tf_op jit(solution)/shard_map/jit(cholesky)/cholesky | solution.py:29
  384.0 9.8 %custom-call.101 = f32[1,128,128]{1,2,0:T(8,128)S(1)} custom-call(f32[1,128,128]{2,1,0:T(8,128)S(1)} %get-tuple-element.611), custom_call_target="InvertDiagBlocksLowerTriangular" | custom-call | tf_op jit(solution)/shard_map/jit(cholesky)/cholesky | solution.py:29
  394.2 5.8 cholesky.822
  402.8 20.1 %custom-call.103 = f32[2,128,128]{1,2,0:T(8,128)S(1)} custom-call(f32[2,128,128]{2,1,0:T(8,128)S(1)} %pad_maximum_fusion.71), custom_call_target="InvertDiagBlocksLowerTriangular" | custom-call | tf_op jit(solution)/shard_map/jit(_solve_triangular)/triangular_solve | solution.py:32
  431.9 3.7 collective-permute-start.5
  442.5 19.8 %collective-permute-done.18 = f32[384]{0:T(512)S(1)} collective-permute-done((f32[384]{0:T(512)S(1)}, f32[384]{0:T(512)S(1)}, u32[]{:S(2)}, u32[]{:S(2)}) %collective-permute-start.18) | collective-permute-done | bytes 1568 | tf_op jit(solution)/shard_map/ppermute | solution.py:24
  463.4 11.7 %cholesky.840 = f32[128,128]{1,0:T(8,128)S(1)} custom-call(f32[128,128]{1,0:T(8,128)S(1)} %cholesky.1003), custom_call_target="Cholesky" | custom-call | tf_op jit(solution)/shard_map/jit(cholesky)/cholesky | solution.py:29
  475.2 9.8 %custom-call.104 = f32[1,128,128]{1,2,0:T(8,128)S(1)} custom-call(f32[1,128,128]{2,1,0:T(8,128)S(1)} %get-tuple-element.609), custom_call_target="InvertDiagBlocksLowerTriangular" | custom-call | tf_op jit(solution)/shard_map/jit(cholesky)/cholesky | solution.py:29
  485.4 5.8 cholesky.860
  494.0 19.9 %custom-call.106 = f32[2,128,128]{1,2,0:T(8,128)S(1)} custom-call(f32[2,128,128]{2,1,0:T(8,128)S(1)} %pad_maximum_fusion.72), custom_call_target="InvertDiagBlocksLowerTriangular" | custom-call | tf_op jit(solution)/shard_map/jit(_solve_triangular)/triangular_solve | solution.py:32
  518.0 3.4 scatter-add.76
  525.1 4.6 collective-permute-start.6
  533.4 4.8 collective-permute-start.19
  538.8 19.7 %collective-permute-done.19 = f32[384]{0:T(512)S(1)} collective-permute-done((f32[384]{0:T(512)S(1)}, f32[384]{0:T(512)S(1)}, u32[]{:S(2)}, u32[]{:S(2)}) %collective-permute-start.19) | collective-permute-done | bytes 1568 | tf_op jit(solution)/shard_map/ppermute | solution.py:24
  559.6 11.7 %cholesky.878 = f32[128,128]{1,0:T(8,128)S(1)} custom-call(f32[128,128]{1,0:T(8,128)S(1)} %cholesky.1006), custom_call_target="Cholesky" | custom-call | tf_op jit(solution)/shard_map/jit(cholesky)/cholesky | solution.py:29
  571.4 9.8 %custom-call.107 = f32[1,128,128]{1,2,0:T(8,128)S(1)} custom-call(f32[1,128,128]{2,1,0:T(8,128)S(1)} %get-tuple-element.607), custom_call_target="InvertDiagBlocksLowerTriangular" | custom-call | tf_op jit(solution)/shard_map/jit(cholesky)/cholesky | solution.py:29
  581.6 5.8 cholesky.898
  590.1 20.1 %custom-call.109 = f32[2,128,128]{1,2,0:T(8,128)S(1)} custom-call(f32[2,128,128]{2,1,0:T(8,128)S(1)} %pad_maximum_fusion.73), custom_call_target="InvertDiagBlocksLowerTriangular" | custom-call | tf_op jit(solution)/shard_map/jit(_solve_triangular)/triangular_solve | solution.py:32
  626.7 3.5 collective-permute-start.20
  630.8 6.6 collective-permute-done.20
  639.1 11.7 %cholesky.916 = f32[128,128]{1,0:T(8,128)S(1)} custom-call(f32[128,128]{1,0:T(8,128)S(1)} %cholesky.1009), custom_call_target="Cholesky" | custom-call | tf_op jit(solution)/shard_map/jit(cholesky)/cholesky | solution.py:29
  650.9 9.8 %custom-call.110 = f32[1,128,128]{1,2,0:T(8,128)S(1)} custom-call(f32[1,128,128]{2,1,0:T(8,128)S(1)} %get-tuple-element.605), custom_call_target="InvertDiagBlocksLowerTriangular" | custom-call | tf_op jit(solution)/shard_map/jit(cholesky)/cholesky | solution.py:29
  661.1 5.8 cholesky.936
  669.7 19.9 %custom-call.112 = f32[2,128,128]{1,2,0:T(8,128)S(1)} custom-call(f32[2,128,128]{2,1,0:T(8,128)S(1)} %pad_maximum_fusion.74), custom_call_target="InvertDiagBlocksLowerTriangular" | custom-call | tf_op jit(solution)/shard_map/jit(_solve_triangular)/triangular_solve | solution.py:32
  707.3 4.3 collective-permute-start.21
  712.2 5.6 collective-permute-done.21
  719.5 11.7 %cholesky.954 = f32[128,128]{1,0:T(8,128)S(1)} custom-call(f32[128,128]{1,0:T(8,128)S(1)} %cholesky.1012), custom_call_target="Cholesky" | custom-call | tf_op jit(solution)/shard_map/jit(cholesky)/cholesky | solution.py:29
  731.3 9.8 %custom-call.113 = f32[1,128,128]{1,2,0:T(8,128)S(1)} custom-call(f32[1,128,128]{2,1,0:T(8,128)S(1)} %get-tuple-element.603), custom_call_target="InvertDiagBlocksLowerTriangular" | custom-call | tf_op jit(solution)/shard_map/jit(cholesky)/cholesky | solution.py:29
  741.5 5.8 cholesky.974
  750.2 20.1 %custom-call.115 = f32[2,128,128]{1,2,0:T(8,128)S(1)} custom-call(f32[2,128,128]{2,1,0:T(8,128)S(1)} %pad_maximum_fusion.75), custom_call_target="InvertDiagBlocksLowerTriangular" | custom-call | tf_op jit(solution)/shard_map/jit(_solve_triangular)/triangular_solve | solution.py:32
  774.5 3.4 scatter-add.86
  783.9 11.7 %cholesky.161 = f32[128,128]{1,0:T(8,128)S(1)} custom-call(f32[128,128]{1,0:T(8,128)S(1)} %cholesky.1015), custom_call_target="Cholesky" | custom-call | tf_op jit(solution)/shard_map/jit(cholesky)/cholesky | solution.py:84
  801.0 10.6 %custom-call.46 = f32[1,128,128]{1,2,0:T(8,128)S(1)} custom-call(f32[1,128,128]{2,1,0:T(8,128)} %get-tuple-element.601), custom_call_target="InvertDiagBlocksLowerTriangular" | custom-call | tf_op jit(solution)/shard_map/jit(cholesky)/cholesky | solution.py:84
  812.3 11.7 %cholesky.248 = f32[128,128]{1,0:T(8,128)S(1)} custom-call(f32[128,128]{1,0:T(8,128)S(1)} %cholesky.1019), custom_call_target="Cholesky" | custom-call | tf_op jit(solution)/shard_map/jit(cholesky)/cholesky | solution.py:84
  824.0 10.0 %custom-call.47 = f32[1,128,128]{1,2,0:T(8,128)S(1)} custom-call(f32[1,128,128]{2,1,0:T(8,128)S(1)} %get-tuple-element.598), custom_call_target="InvertDiagBlocksLowerTriangular" | custom-call | tf_op jit(solution)/shard_map/jit(cholesky)/cholesky | solution.py:84
  834.5 11.7 %cholesky.267 = f32[128,128]{1,0:T(8,128)S(1)} custom-call(f32[128,128]{1,0:T(8,128)S(1)} %convolution_subtract_fusion.10), custom_call_target="Cholesky" | custom-call | tf_op jit(solution)/shard_map/jit(cholesky)/cholesky | solution.py:84
  851.2 7.7 while.59
  858.9 30.3 %custom-call.48 = f32[3,128,128]{1,2,0:T(8,128)S(1)} custom-call(f32[3,128,128]{2,1,0:T(8,128)} %get-tuple-element.265), custom_call_target="InvertDiagBlocksLowerTriangular" | custom-call | tf_op jit(solution)/shard_map/jit(_solve_triangular)/triangular_solve | solution.py:86
  (629 shorter events, 208.3 us)
Async XLA Ops:
  0.0 27.3 %copy-start = (f32[1,6,8,256]{3,2,1,0:T(8,128)S(1)}, f32[1,6,8,256]{3,2,1,0:T(8,128)}, u32[]{:S(2)}) copy-start(f32[1,6,8,256]{3,2,1,0:T(8,128)} %param.56) | copy-start | bytes 147460
  0.0 10.2 %copy-start.1 = (f32[1,64,8,256]{3,2,1,0:T(8,128)S(1)}, f32[1,64,8,256]{3,2,1,0:T(8,128)}, u32[]{:S(2)}) copy-start(f32[1,64,8,256]{3,2,1,0:T(8,128)} %param.52) | copy-start | bytes 1572868
  1.4 30.1 %collective-permute-start = (f32[384,384]{0,1:T(8,128)S(1)}, f32[384,384]{0,1:T(8,128)S(1)}, u32[]{:S(2)}, u32[]{:S(2)}) collective-permute-start(f32[384,384]{0,1:T(8,128)S(1)} %bitcast.914), channel_id=1, source_target_pairs={{0,1},{1,0},{2,3},{3,2},{4,5},{5,4},{6,7},{7,6},{8,9},{9,8},{10,11... | collective-permute-start | bytes 1769480 | tf_op jit(solution)/shard_map/ppermute | solution.py:24
  11.1 10.1 %collective-permute-start.12 = (f32[1,64,8,1]{3,1,2,0:T(8,128)}, f32[1,64,8,1]{3,1,2,0:T(8,128)}, u32[]{:S(2)}, u32[]{:S(2)}) collective-permute-start(f32[1,64,8,1]{3,1,2,0:T(8,128)} %get-tuple-element.567), channel_id=1, source_target_pairs={{2,0},{4,2},{6,4},{8,6},{10,8},{12,10},{14,12},{0,14},{3,1},{5,3},... | collective-permute-start | bytes 6152 | tf_op jit(solution)/shard_map/ppermute | solution.py:18
  13.0 11.1 %collective-permute-start.11 = (f32[1,64,8,1]{3,1,2,0:T(8,128)S(1)}, f32[1,64,8,1]{3,1,2,0:T(8,128)}, u32[]{:S(2)}, u32[]{:S(2)}) collective-permute-start(f32[1,64,8,1]{3,1,2,0:T(8,128)S(1)} %get-tuple-element.566), channel_id=1, source_target_pairs={{0,2},{2,4},{4,6},{6,8},{8,10},{10,12},{12,14},{14,0},{1,3},{3,5},... | collective-permute-start | bytes 6152 | tf_op jit(solution)/shard_map/ppermute | solution.py:17
  16.4 7.7 collective-permute-start.10
  17.7 6.5 collective-permute-start.9
  20.5 3.7 copy-start.42
  27.9 3.5 collective-permute-start.13
  92.4 17.2 %collective-permute-start.1 = (f32[384,384]{0,1:T(8,128)S(1)}, f32[384,384]{0,1:T(8,128)S(1)}, u32[]{:S(2)}, u32[]{:S(2)}) collective-permute-start(f32[384,384]{0,1:T(8,128)S(1)} %scatter-add.61), channel_id=1, source_target_pairs={{0,2},{1,3},{2,0},{3,1},{4,6},{5,7},{6,4},{7,5},{8,10},{9,11},{10,... | collective-permute-start | bytes 1769480 | tf_op jit(solution)/shard_map/ppermute | solution.py:24
  95.2 13.7 %collective-permute-start.14 = (f32[384]{0:T(512)S(1)}, f32[384]{0:T(512)S(1)}, u32[]{:S(2)}, u32[]{:S(2)}) collective-permute-start(f32[384]{0:T(512)S(1)} %fusion.239), channel_id=1, source_target_pairs={{0,2},{1,3},{2,0},{3,1},{4,6},{5,7},{6,4},{7,5},{8,10},{9,11},{10,... | collective-permute-start | bytes 4616 | tf_op jit(solution)/shard_map/ppermute | solution.py:24
  169.4 3.1 copy-start.44
  169.5 30.8 %collective-permute-start.2 = (f32[384,384]{0,1:T(8,128)S(1)}, f32[384,384]{0,1:T(8,128)S(1)}, u32[]{:S(2)}, u32[]{:S(2)}) collective-permute-start(f32[384,384]{0,1:T(8,128)S(1)} %scatter-add.65), channel_id=1, source_target_pairs={{0,4},{1,5},{2,6},{3,7},{4,0},{5,1},{6,2},{7,3},{8,12},{9,13},{10,... | collective-permute-start | bytes 1769480 | tf_op jit(solution)/shard_map/ppermute | solution.py:24
  174.7 25.5 %collective-permute-start.15 = (f32[384]{0:T(512)S(1)}, f32[384]{0:T(512)S(1)}, u32[]{:S(2)}, u32[]{:S(2)}) collective-permute-start(f32[384]{0:T(512)S(1)} %fusion.240), channel_id=1, source_target_pairs={{0,4},{1,5},{2,6},{3,7},{4,0},{5,1},{6,2},{7,3},{8,12},{9,13},{10,... | collective-permute-start | bytes 4616 | tf_op jit(solution)/shard_map/ppermute | solution.py:24
  231.4 21.8 %copy-start.36 = (f32[192,192]{1,0:T(8,128)}, f32[192,192]{1,0:T(8,128)S(1)}, u32[]{:S(2)}) copy-start(f32[192,192]{1,0:T(8,128)S(1)} %select_select_fusion.7) | copy-start | bytes 442372
  260.5 34.3 %collective-permute-start.3 = (f32[384,384]{0,1:T(8,128)S(1)}, f32[384,384]{0,1:T(8,128)S(1)}, u32[]{:S(2)}, u32[]{:S(2)}) collective-permute-start(f32[384,384]{0,1:T(8,128)S(1)} %scatter-add.69), channel_id=1, source_target_pairs={{0,8},{1,9},{2,10},{3,11},{4,12},{5,13},{6,14},{7,15},{8,0},{9,1},... | collective-permute-start | bytes 1769480 | tf_op jit(solution)/shard_map/ppermute | solution.py:24
  268.4 25.7 %collective-permute-start.16 = (f32[384]{0:T(512)S(1)}, f32[384]{0:T(512)S(1)}, u32[]{:S(2)}, u32[]{:S(2)}) collective-permute-start(f32[384]{0:T(512)S(1)} %fusion.241), channel_id=1, source_target_pairs={{0,8},{1,9},{2,10},{3,11},{4,12},{5,13},{6,14},{7,15},{8,0},{9,1},... | collective-permute-start | bytes 4616 | tf_op jit(solution)/shard_map/ppermute | solution.py:24
  325.8 21.6 %copy-start.37 = (f32[192,192]{1,0:T(8,128)}, f32[192,192]{1,0:T(8,128)S(1)}, u32[]{:S(2)}) copy-start(f32[192,192]{1,0:T(8,128)S(1)} %select_select_fusion.6) | copy-start | bytes 442372
  354.7 1.9 copy-start.45
  354.7 17.0 %collective-permute-start.4 = (f32[384,384]{0,1:T(8,128)S(1)}, f32[384,384]{0,1:T(8,128)S(1)}, u32[]{:S(2)}, u32[]{:S(2)}) collective-permute-start(f32[384,384]{0,1:T(8,128)S(1)} %scatter-add.71), channel_id=1, source_target_pairs={{0,16},{1,17},{2,18},{3,19},{4,20},{5,21},{6,22},{7,23},{8,24},{9,... | collective-permute-start | bytes 1769480 | tf_op jit(solution)/shard_map/ppermute | solution.py:24
  360.3 10.7 %collective-permute-start.17 = (f32[384]{0:T(512)S(1)}, f32[384]{0:T(512)S(1)}, u32[]{:S(2)}, u32[]{:S(2)}) collective-permute-start(f32[384]{0:T(512)S(1)} %fusion.242), channel_id=1, source_target_pairs={{0,16},{1,17},{2,18},{3,19},{4,20},{5,21},{6,22},{7,23},{8,24},{9,... | collective-permute-start | bytes 4616 | tf_op jit(solution)/shard_map/ppermute | solution.py:24
  402.7 21.9 %copy-start.38 = (f32[192,192]{1,0:T(8,128)}, f32[192,192]{1,0:T(8,128)S(1)}, u32[]{:S(2)}) copy-start(f32[192,192]{1,0:T(8,128)S(1)} %select_select_fusion.5) | copy-start | bytes 442372
  423.0 2.0 copy-start.27
  429.6 6.0 copy-start.28
  431.9 3.7 copy-start.46
  431.9 31.1 %collective-permute-start.5 = (f32[384,384]{0,1:T(8,128)S(1)}, f32[384,384]{0,1:T(8,128)S(1)}, u32[]{:S(2)}, u32[]{:S(2)}) collective-permute-start(f32[384,384]{0,1:T(8,128)S(1)} %scatter-add.75), channel_id=1, source_target_pairs={{0,32},{1,33},{2,34},{3,35},{4,36},{5,37},{6,38},{7,39},{8,40},{9,... | collective-permute-start | bytes 1769480 | tf_op jit(solution)/shard_map/ppermute | solution.py:24
  439.3 23.0 %collective-permute-start.18 = (f32[384]{0:T(512)S(1)}, f32[384]{0:T(512)S(1)}, u32[]{:S(2)}, u32[]{:S(2)}) collective-permute-start(f32[384]{0:T(512)S(1)} %fusion.243), channel_id=1, source_target_pairs={{0,32},{1,33},{2,34},{3,35},{4,36},{5,37},{6,38},{7,39},{8,40},{9,... | collective-permute-start | bytes 4616 | tf_op jit(solution)/shard_map/ppermute | solution.py:24
  493.9 21.6 %copy-start.39 = (f32[192,192]{1,0:T(8,128)}, f32[192,192]{1,0:T(8,128)S(1)}, u32[]{:S(2)}) copy-start(f32[192,192]{1,0:T(8,128)S(1)} %select_select_fusion.4) | copy-start | bytes 442372
  513.9 2.0 copy-start.29
  522.1 7.6 copy-start.30
  525.1 4.6 copy-start.47
  525.1 34.0 %collective-permute-start.6 = (f32[384,384]{0,1:T(8,128)S(1)}, f32[384,384]{0,1:T(8,128)S(1)}, u32[]{:S(2)}, u32[]{:S(2)}) collective-permute-start(f32[384,384]{0,1:T(8,128)S(1)} %scatter-add.79), channel_id=1, source_target_pairs={{0,64},{1,65},{2,66},{3,67},{4,68},{5,69},{6,70},{7,71},{8,72},{9,... | collective-permute-start | bytes 1769480 | tf_op jit(solution)/shard_map/ppermute | solution.py:24
  533.4 25.1 %collective-permute-start.19 = (f32[384]{0:T(512)S(1)}, f32[384]{0:T(512)S(1)}, u32[]{:S(2)}, u32[]{:S(2)}) collective-permute-start(f32[384]{0:T(512)S(1)} %fusion.244), channel_id=1, source_target_pairs={{0,64},{1,65},{2,66},{3,67},{4,68},{5,69},{6,70},{7,71},{8,72},{9,... | collective-permute-start | bytes 4616 | tf_op jit(solution)/shard_map/ppermute | solution.py:24
  559.1 53.5 %copy-start.6 = (f32[384,384]{0,1:T(8,128)}, f32[384,384]{0,1:T(8,128)S(1)}, u32[]{:S(2)}) copy-start(f32[384,384]{0,1:T(8,128)S(1)} %collective-permute-done.6) | copy-start | bytes 1769476
  590.0 21.9 %copy-start.40 = (f32[192,192]{1,0:T(8,128)}, f32[192,192]{1,0:T(8,128)S(1)}, u32[]{:S(2)}) copy-start(f32[192,192]{1,0:T(8,128)S(1)} %select_select_fusion.3) | copy-start | bytes 442372
  610.3 2.0 copy-start.31
  618.8 4.2 copy-start.32
  621.1 2.0 copy-start.48
  621.1 17.0 %collective-permute-start.7 = (f32[384,384]{0,1:T(8,128)S(1)}, f32[384,384]{0,1:T(8,128)S(1)}, u32[]{:S(2)}, u32[]{:S(2)}) collective-permute-start(f32[384,384]{0,1:T(8,128)S(1)} %scatter-add.81), channel_id=1, source_target_pairs={{0,128},{1,129},{2,130},{3,131},{4,132},{5,133},{6,134},{7,135},{8... | collective-permute-start | bytes 1769480 | tf_op jit(solution)/shard_map/ppermute | solution.py:24
  626.7 10.7 %collective-permute-start.20 = (f32[384]{0:T(512)S(1)}, f32[384]{0:T(512)S(1)}, u32[]{:S(2)}, u32[]{:S(2)}) collective-permute-start(f32[384]{0:T(512)S(1)} %fusion.245), channel_id=1, source_target_pairs={{0,128},{1,129},{2,130},{3,131},{4,132},{5,133},{6,134},{7,135},{8... | collective-permute-start | bytes 4616 | tf_op jit(solution)/shard_map/ppermute | solution.py:24
  638.1 0.8 copy-start.7
  669.5 21.6 %copy-start.41 = (f32[192,192]{1,0:T(8,128)}, f32[192,192]{1,0:T(8,128)S(1)}, u32[]{:S(2)}) copy-start(f32[192,192]{1,0:T(8,128)S(1)} %select_select_fusion.2) | copy-start | bytes 442372
  689.6 2.0 copy-start.33
  690.9 1.1 copy-start.8
  691.1 0.9 copy-start.21
  697.9 5.7 copy-start.34
  700.9 2.7 copy-start.49
  700.9 17.6 %collective-permute-start.8 = (f32[384,384]{0,1:T(8,128)S(1)}, f32[384,384]{0,1:T(8,128)S(1)}, u32[]{:S(2)}, u32[]{:S(2)}) collective-permute-start(f32[384,384]{0,1:T(8,128)S(1)} %scatter-add.85), channel_id=1, source_target_pairs={{0,256},{1,257},{2,258},{3,259},{4,260},{5,261},{6,262},{7,263},{8... | collective-permute-start | bytes 1769480 | tf_op jit(solution)/shard_map/ppermute | solution.py:24
  707.3 10.5 %collective-permute-start.21 = (f32[384]{0:T(512)S(1)}, f32[384]{0:T(512)S(1)}, u32[]{:S(2)}, u32[]{:S(2)}) collective-permute-start(f32[384]{0:T(512)S(1)} %fusion.246), channel_id=1, source_target_pairs={{0,256},{1,257},{2,258},{3,259},{4,260},{5,261},{6,262},{7,263},{8... | collective-permute-start | bytes 4616 | tf_op jit(solution)/shard_map/ppermute | solution.py:24
  750.0 21.9 %copy-start.35 = (f32[192,192]{1,0:T(8,128)}, f32[192,192]{1,0:T(8,128)S(1)}, u32[]{:S(2)}) copy-start(f32[192,192]{1,0:T(8,128)S(1)} %select_select_fusion.1) | copy-start | bytes 442372
  770.3 2.0 copy-start.25
  771.6 1.1 copy-start.5
  771.9 0.9 copy-start.23
  795.6 16.1 %copy-start.3 = (f32[384,384]{1,0:T(8,128)S(1)}, f32[384,384]{1,0:T(8,128)}, u32[]{:S(2)}) copy-start(f32[384,384]{1,0:T(8,128)} %copy-done.2) | copy-start | bytes 1769476
  795.7 1.2 copy-start.26
  851.2 38.0 %copy-start.57 = (f32[192]{0:T(256)S(1)}, f32[192]{0:T(256)}, u32[]{:S(2)}) copy-start(f32[192]{0:T(256)} %get-tuple-element.642) | copy-start | bytes 2308
  891.5 0.9 copy-start.24
  892.4 0.9 copy-start.22
  893.3 1.2 copy-start.20
  894.5 1.2 copy-start.18
  895.7 1.2 copy-start.16
  896.8 1.1 copy-start.14
  898.0 1.1 copy-start.12
  899.1 1.2 copy-start.10
  (35 other events, 24.6 us)
where the time goes:
time: 918 us; the launch traced here: 903 us
  other arithmetic  553 us (60%)
  waiting for transfers between devices  114 us (12%)
  local copies, waits for them, and re-layouts  80.9 us (9%)
  starting transfers between devices  74.3 us (8%)
  matrix products  65.1 us (7%)
  between operations  16.3 us (2%)
    another operation x63, other arithmetic, eliminate(): factor = jnp.linalg.cholesky(shared_sum)  259 us
    another operation x38, other arithmetic, eliminate(): jax.scipy.linalg.solve_triangular(factor, inner, lower=True, trans=1)  181 us
    ppermute x18, waiting for transfers between devices, partner(): lax.ppermute(array, axis, [(i, i ^ 1 << distance) for i in range(lax.axis...  111 us
    ppermute x18, starting transfers between devices, partner(): lax.ppermute(array, axis, [(i, i ^ 1 << distance) for i in range(lax.axis...  66.5 us
    another operation x11, other arithmetic, body(): root_factor = jnp.linalg.cholesky(schur)  58.9 us
    another operation x3, other arithmetic, body(): jax.scipy.linalg.solve_triangular(root_factor, inner, lower=True, trans=1)  30.9 us
    scatter-add x9, local copies, waits for them, and re-layouts, body(): parent = parent.at[:middle, :middle].add(first_outer)  28.7 us
    scatter-add x10, local copies, waits for them, and re-layouts, body(): parent = parent.at[middle:, middle:].add(second_outer)  22.8 us
  transfers between devices with their start and end apart: 22, of which 11 were waited for; matrix products, arithmetic and copies ran while one was open for 4% of the time, Pallas kernels for 0%

commit v1 on v0

v1 whole, which is shorter than its diff:
```python
import functools

import jax
import jax.numpy as jnp
from jax import lax
from jax.experimental import pallas as pl
from jax.experimental.pallas import tpu as pltpu
from jax.sharding import PartitionSpec as P

highest = lax.Precision.HIGHEST
diffusion = 0.5
F32 = jnp.float32
MESH = pl.DeviceIdType.MESH
H = 192
A = 128
B = 64


def extended(array, sides, width, wrap):
    for axis, dim in sides:
        size, length = (lax.axis_size(axis), array.shape[dim])
        up = [(i, (i + 1) % size) for i in range(size if wrap else size - 1)]
        down = [(j, i) for i, j in up]
        last = lax.slice_in_dim(array, length - width, length, axis=dim)
        first = lax.slice_in_dim(array, 0, width, axis=dim)
        before = lax.ppermute(last, axis, up)
        after = lax.ppermute(first, axis, down)
        array = jnp.concatenate([before, array, after], axis=dim)
    return array


def mm(a, b):
    return lax.dot_general(a, b, (((1,), (0,)), ((), ())), precision=highest, preferred_element_type=F32)


def mtn(a, b):
    return lax.dot_general(a, b, (((0,), (0,)), ((), ())), precision=highest, preferred_element_type=F32)


def mnt(a, b):
    return lax.dot_general(a, b, (((1,), (1,)), ((), ())), precision=highest, preferred_element_type=F32)


def row_of(x, i):
    return jnp.broadcast_to(x[i : i + 1, :], x.shape)


def col_of(x, i):
    return jnp.broadcast_to(x[:, i : i + 1], x.shape)


def tree_sum(terms):
    terms = list(terms)
    while len(terms) > 1:
        terms = [terms[i] + terms[i + 1] if i + 1 < len(terms) else terms[i] for i in range(0, len(terms), 2)]
    return terms[0]


def invert8(columns):
    sub = lax.broadcasted_iota(jnp.int32, (8, 128), 0)
    columns = list(columns)
    for p in range(0, 8, 2):
        x, y = columns[p], columns[p + 1]
        a, b, c = row_of(x, p), row_of(y, p), row_of(y, p + 1)
        scale = 1.0 / (a * c - b * b)
        first, second = sub == p, sub == p + 1
        pivot_rows = jnp.logical_or(first, second)
        hu = jnp.where(first, c, jnp.where(second, -b, y * b - x * c))
        hv = jnp.where(first, -b, jnp.where(second, a, x * b - y * a))
        for j in range(8):
            if j in (p, p + 1):
                continue
            u, v = row_of(columns[j], p), row_of(columns[j], p + 1)
            columns[j] = jnp.where(pivot_rows, 0.0, columns[j]) + (hu * u + hv * v) * scale
        columns[p] = hu * scale
        columns[p + 1] = hv * scale
    return columns


def gauss_jordan(tiles, n):
    count, parts = len(tiles), len(tiles[0])
    sub = lax.broadcasted_iota(jnp.int32, (8, 128), 0)
    lane = lax.broadcasted_iota(jnp.int32, (8, 128), 1)
    for k in range(n // 8):
        part, start = (8 * k) // 128, (8 * k) % 128
        block = jnp.logical_and(lane >= start, lane < start + 8)
        inverse = invert8([col_of(tiles[k][part], start + j) for j in range(8)])
        pivot = []
        for l in range(parts):
            value = tiles[k][l]
            if l == part:
                value = jnp.where(block, jnp.where(lane - start == sub, 1.0, 0.0), value)
            pivot.append(tree_sum([inverse[j] * row_of(value, j) for j in range(8)]))
        rows = [[row_of(pivot[l], j) for j in range(8)] for l in range(parts)]
        for i in [i % count for i in range(k + 1, k + count)]:
            factors = [col_of(tiles[i][part], start + j) for j in range(8)]
            fresh = []
            for l in range(parts):
                base = tiles[i][l]
                if l == part:
                    base = jnp.where(block, 0.0, base)
                fresh.append(base - tree_sum([factors[j] * rows[l][j] for j in range(8)]))
            tiles[i] = fresh
        tiles[k] = pivot
    return tiles


def tree_kernel(
    sizes, leaf_ref, rhs_ref, out_ref, ssb, eb, oob, fb, ainv, yb, sc, xs, zs, xv, up_send, up_recv, down_send, down_recv
):
    n_axial, n_azim, n_bank = sizes
    total = n_axial * n_azim * n_bank
    merges = total.bit_length() - 1
    me = (lax.axis_index("axial") * n_azim + lax.axis_index("azim")) * n_bank + lax.axis_index("bank")

    def device(n):
        return (n // (n_azim * n_bank), (n // n_bank) % n_azim, n % n_bank)

    def step_of(level):
        if isinstance(level, int):
            return 1 << (level if level < merges else merges - 1)
        step = jnp.int32(1)
        for l in range(1, merges + 1):
            step = jnp.where(level == l, jnp.int32(1 << (l if l < merges else merges - 1)), step)
        return step

    def receives(level):
        return jnp.logical_and(level != merges - 1, me % (2 * step_of(level)) == 0)

    def sends(level):
        step = step_of(level)
        return jnp.logical_and(level != merges - 1, me % (2 * step) == step)

    def computes(level):
        return jnp.where(level == merges - 1, me % step_of(level) == 0, me % (2 * step_of(level)) == 0)

    pieces = (ssb, eb, oob, fb)

    def upward(level, which):
        ref = pieces[which]
        return pltpu.make_async_remote_copy(
            src_ref=ref.at[level, 0],
            dst_ref=ref.at[level, 1],
            send_sem=up_send.at[which],
            recv_sem=up_recv.at[level, which],
            device_id=device(me - step_of(level)),
            device_id_type=MESH,
        )

    def downward(level, peer):
        return pltpu.make_async_remote_copy(
            src_ref=xv.at[level, 1],
            dst_ref=xv.at[level, 0],
            send_sem=down_send.at[level],
            recv_sem=down_recv.at[level],
            device_id=device(peer),
            device_id_type=MESH,
        )

    barrier = pltpu.get_barrier_semaphore()
    levels = [l for l in range(merges + 1) if l != merges - 1]
    for level in levels:
        step = step_of(level)

        @pl.when(me % step == 0)
        def _():
            peer = jnp.where(me % (2 * step) == 0, me + step, me - step)
            pl.semaphore_signal(barrier, inc=1, device_id=device(peer), device_id_type=MESH)

    def put_ss(level, value):
        ssb[level, 0, :, 0:A] = value[0:A, 0:A]
        ssb[level, 0, 0:B, A : 2 * A] = jnp.concatenate([value[0:B, A:H], value[A:H, A:H]], axis=1)
        ssb[level, 0, B:A, A : 2 * A] = jnp.concatenate([value[B:A, A:H], jnp.zeros((A - B, B), F32)], axis=1)

    put_ss(0, leaf_ref[H:, H:])
    eb[0, 0] = leaf_ref[H:, :H]
    oob[0, 0] = leaf_ref[:H, :H]
    fb[0, 0, 0] = jnp.broadcast_to(rhs_ref[:, :H], (8, H))
    fb[0, 0, 1] = jnp.broadcast_to(rhs_ref[:, H:], (8, H))
    local = merges - 1
    ssb[local, 1] = jnp.zeros((A, 2 * A), F32)
    eb[local, 1] = jnp.zeros((H, H), F32)
    oob[local, 1] = jnp.zeros((H, H), F32)
    fb[local, 1] = jnp.zeros((2, 8, H), F32)
    sc[...] = jnp.zeros((B, 2 * B), F32)

    peers = jnp.int32(0)
    for level in levels:
        peers = peers + jnp.where(me % step_of(level) == 0, 1, 0)
    pl.semaphore_wait(barrier, peers)

    @pl.when(sends(0))
    def _():
        for which in range(4):
            upward(0, which).start()

    def ascend(level, carry):
        @pl.when(computes(level))
        def _():
            first = jnp.where(level >= merges - 2, jnp.where(level == merges, 0, 1), 0)
            second = 1 - first

            @pl.when(level != local)
            def _():
                upward(level, 0).wait_recv()

            tiles = []
            for i in range(A // 8):
                tiles.append(
                    [
                        ssb[level, 0, 8 * i : 8 * i + 8, 128 * l : 128 * l + 128]
                        + ssb[level, 1, 8 * i : 8 * i + 8, 128 * l : 128 * l + 128]
                        for l in range(2)
                    ]
                )
            tiles = gauss_jordan(tiles, A)
            for i in range(A // 8):
                ainv[8 * i : 8 * i + 8, :] = tiles[i][0]
                yb[8 * i : 8 * i + 8, :] = tiles[i][1][:, 0:B]

            @pl.when(level != local)
            def _():
                for which in range(1, 4):
                    upward(level, which).wait_recv()

            y = yb[...]
            bc = ssb[level, 0, :, A : 2 * A] + ssb[level, 1, :, A : 2 * A]
            corner = bc[0:B, B : 2 * B] - mtn(bc[:, 0:B], y)
            sc[:, 0:B] = corner
            low = [[sc[8 * i : 8 * i + 8, :]] for i in range(B // 8)]
            low = gauss_jordan(low, B)
            e = [eb[level, first], eb[level, second]]
            inverse_a = ainv[...]
            g = [mm(inverse_a, e[q][0:A]) for q in range(2)]
            t = [e[q][A:H] - mtn(y, e[q][0:A]) for q in range(2)]
            for i in range(B // 8):
                sc[8 * i : 8 * i + 8, :] = low[i][0]
            inverse_s = sc[:, 0:B]
            x2 = [mm(inverse_s, t[q]) for q in range(2)]
            ss = oob[level, second] - mtn(e[1][0:A], g[1]) - mtn(t[1], x2[1])
            put_ss(level + 1, ss)

            @pl.when(jnp.logical_and(level < merges, sends(level + 1)))
            def _():
                upward(level + 1, 0).start()

            eb[level + 1, 0] = -mtn(e[1][0:A], g[0]) - mtn(t[1], x2[0])
            oob[level + 1, 0] = oob[level, first] - mtn(e[0][0:A], g[0]) - mtn(t[0], x2[0])
            for q in range(2):
                xs[level, q, 0:A] = g[q] - mm(y, x2[q])
                xs[level, q, A:H] = x2[q]
            shared = fb[level, 0, 1] + fb[level, 1, 1]
            tail = shared[:, A:H] - mm(shared[:, 0:A], y)
            z2 = mm(tail, inverse_s)
            z1 = mm(shared[:, 0:A], inverse_a) - mnt(z2, y)
            zs[level, :, 0:A] = z1
            zs[level, :, A:H] = z2
            for q, slot in ((0, first), (1, second)):
                fb[level + 1, 0, q] = fb[level, slot, 0] - mm(z1, e[q][0:A]) - mm(z2, e[q][A:H])

            @pl.when(jnp.logical_and(level < merges, sends(level + 1)))
            def _():
                for which in range(1, 4):
                    upward(level + 1, which).start()

        return carry

    lax.fori_loop(0, merges + 1, ascend, 0)

    xv[merges + 1, 0] = jnp.zeros((2, 8, H), F32)

    def descend(i, carry):
        level = merges - i

        @pl.when(sends(level))
        def _():
            for which in range(4):
                upward(level, which).wait_send()
            downward(level, me).wait_recv()

        @pl.when(computes(level))
        def _():
            above = level + 1
            first = jnp.where(level >= merges - 2, jnp.where(level == merges, 0, 1), 0)
            y = zs[level] - mnt(xv[above, 0, 0], xs[level, 0]) - mnt(xv[above, 0, 1], xs[level, 1])
            xv[level, 0, 0] = xv[above, 0, first]
            xv[level, 0, 1] = y
            xv[level, 1, 0] = xv[above, 0, 1 - first]
            xv[level, 1, 1] = y

            @pl.when(level != local)
            def _():
                downward(level, me + step_of(level)).start()

        return carry

    lax.fori_loop(0, merges + 1, descend, 0)
    out_ref[:, 0:H] = xv[0, 0, 0, 0:1]
    out_ref[:, H:] = xv[0, 0, 1, 0:1]

    def finish(level, carry):
        @pl.when(receives(level))
        def _():
            downward(level, me + step_of(level)).wait_send()

        return carry

    lax.fori_loop(0, merges + 1, finish, 0)


def solve_tree(schur, rhs, sizes):
    total = sizes[0] * sizes[1] * sizes[2]
    slots = total.bit_length() + 1
    vmem = pl.BlockSpec(memory_space=pltpu.VMEM)
    return pl.pallas_call(
        functools.partial(tree_kernel, sizes),
        out_shape=jax.ShapeDtypeStruct((1, 2 * H), F32),
        in_specs=[vmem, vmem],
        out_specs=vmem,
        scratch_shapes=[
            pltpu.VMEM((slots, 2, A, 2 * A), F32),
            pltpu.VMEM((slots, 2, H, H), F32),
            pltpu.VMEM((slots, 2, H, H), F32),
            pltpu.VMEM((slots, 2, 2, 8, H), F32),
            pltpu.VMEM((A, A), F32),
            pltpu.VMEM((A, B), F32),
            pltpu.VMEM((B, 2 * B), F32),
            pltpu.VMEM((slots, 2, H, H), F32),
            pltpu.VMEM((slots, 8, H), F32),
            pltpu.VMEM((slots, 2, 2, 8, H), F32),
            pltpu.SemaphoreType.DMA((4,)),
            pltpu.SemaphoreType.DMA((slots, 4)),
            pltpu.SemaphoreType.DMA((slots,)),
            pltpu.SemaphoreType.DMA((slots,)),
        ],
        compiler_params=pltpu.CompilerParams(
            collective_id=0, has_side_effects=True, vmem_limit_bytes=48 * 1024 * 1024
        ),
    )(schur, rhs)


def leaf_rhs(adjoint_state, adjoint_source, reaction_rate, jacobian, lifting, separator):
    along_axial = extended(adjoint_state, (("axial", 2),), 1, False)
    along_azim = extended(adjoint_state, (("azim", 3),), 1, True)
    scaled = reaction_rate[:, None] * adjoint_state
    reaction = jnp.einsum("bvu,bvxz->buxz", jacobian, scaled, precision=highest)
    neighbours = along_axial[:, :, 2:, :] + along_axial[:, :, :-2, :]
    neighbours = neighbours + along_azim[:, :, :, :-2] + along_azim[:, :, :, 2:]
    residual = adjoint_source - reaction - diffusion * (4.0 * adjoint_state - neighbours)
    chans = residual.shape[1]
    flat_residual = residual.reshape(chans, -1)
    sep_cells = separator.reshape(-1)
    picked = jnp.take(flat_residual, sep_cells, axis=1).T
    lifted = jnp.einsum(
        "ck,vk->cv", lifting.reshape(sep_cells.shape[0], -1), flat_residual, precision=highest
    )
    return (picked + lifted).reshape(1, -1)


def body(sizes, adjoint_state, adjoint_source, reaction_rate, jacobian, lifting, separator, leaf_schur):
    rhs = leaf_rhs(adjoint_state, adjoint_source, reaction_rate, jacobian, lifting, separator)
    answer = solve_tree(leaf_schur.reshape(2 * H, 2 * H), rhs, sizes)
    return answer.reshape(1, 1, 1, 2 * H)


def solution(mesh):
    sizes = (mesh.shape["axial"], mesh.shape["azim"], mesh.shape["bank"])
    in_specs = (
        P("bank", None, "axial", "azim"),
        P("bank", None, "axial", "azim"),
        P("bank", "axial", "azim"),
        P("bank", None, None),
        P("bank", None, "axial", "azim"),
        P("axial", "azim", "bank", None),
        P("axial", "azim", "bank", None, None),
    )
    out_specs = P("axial", "azim", "bank", None)
    return jax.shard_map(
        functools.partial(body, sizes), mesh=mesh, in_specs=in_specs, out_specs=out_specs, check_vma=False
    )
```

time: 918 us -> 177 us (0.19)
  the two profiles are of different devices: /device:TPU:1 before, /device:TPU:511 now
where the time goes in v1:
time: 177 us
  Pallas kernels  160 us (90%)
  starting transfers between devices  8.89 us (5%)
  waiting for transfers between devices  3.86 us (2%)
  local copies, waits for them, and re-layouts  2.95 us (2%)
    pallas_call x1, Pallas kernels, solve_tree(): pl.pallas_call(functools.partial(tree_kernel, sizes), out_shape=jax.Shape...  160 us
    ppermute x2, starting transfers between devices, extended(): after = lax.ppermute(first, axis, down)  5.54 us
  transfers between devices with their start and end apart: 4, of which 3 were waited for; matrix products, arithmetic and copies ran while one was open for 0% of the time, Pallas kernels for 0%

profile of v1, /device:TPU:511, one launch (start us, length us, event | category | flops | bytes accessed | tf_op | source)
XLA Modules:
  0.0 177.0 jit_solution(11493022369227025746)
XLA Ops:
  0.0 0.0 copy-start
  0.0 1.2 copy.24
  1.2 0.0 copy-start.2
  1.2 0.1 fusion.15
  1.4 2.1 %collective-permute-start.2 = (f32[1,64,8,1]{3,1,2,0:T(8,128)S(1)}, f32[1,64,8,1]{3,1,2,0:T(8,128)S(1)}, u32[]{:S(2)}, u32[]{:S(2)}) collective-permute-start(f32[1,64,8,1]{3,1,2,0:T(8,128)S(1)} %get-tuple-element.7), channel_id=1, source_target_pairs={{0,2},{2,4},{4,6},{6,8},{8,10},{10,12},{12,14},{14,0},{1,3},{3,5},... | collective-permute-start | bytes 6152 | tf_op jit(solution)/shard_map/ppermute | solution.py:26
  3.4 3.4 %collective-permute-start.3 = (f32[1,64,8,1]{3,1,2,0:T(8,128)S(1)}, f32[1,64,8,1]{3,1,2,0:T(8,128)S(1)}, u32[]{:S(2)}, u32[]{:S(2)}) collective-permute-start(f32[1,64,8,1]{3,1,2,0:T(8,128)S(1)} %get-tuple-element.8), channel_id=1, source_target_pairs={{2,0},{4,2},{6,4},{8,6},{10,8},{12,10},{14,12},{0,14},{3,1},{5,3},... | collective-permute-start | bytes 6152 | tf_op jit(solution)/shard_map/ppermute | solution.py:27
  6.8 0.0 copy-start.6
  6.8 0.0 copy-start.5
  6.8 2.2 %collective-permute-start = (f32[1,64,1,256]{3,1,2,0:T(8,128)S(1)}, f32[1,64,1,256]{3,1,2,0:T(8,128)S(1)}, u32[]{:S(2)}, u32[]{:S(2)}) collective-permute-start(f32[1,64,1,256]{3,1,2,0:T(8,128)S(1)} %get-tuple-element.5), channel_id=1, source_target_pairs={{16,0},{32,16},{48,32},{64,48},{80,64},{96,80},{112,96},{128,112},... | collective-permute-start | bytes 196616 | tf_op jit(solution)/shard_map/ppermute | solution.py:27
  9.0 1.3 collective-permute-start.1
  10.3 0.0 copy-done.6
  10.4 0.0 copy-done.2
  10.4 0.0 copy-done.5
  10.4 0.0 copy-start.3
  10.4 0.0 copy-start.4
  10.5 0.1 collective-permute-done.2
  10.6 3.1 %collective-permute-done.3 = f32[1,64,8,1]{3,1,2,0:T(8,128)S(1)} collective-permute-done((f32[1,64,8,1]{3,1,2,0:T(8,128)S(1)}, f32[1,64,8,1]{3,1,2,0:T(8,128)S(1)}, u32[]{:S(2)}, u32[]{:S(2)}) %collective-permute-start.3) | collective-permute-done | bytes 2080 | tf_op jit(solution)/shard_map/ppermute | solution.py:27
  13.7 0.0 collective-permute-done
  13.7 0.6 collective-permute-done.1
  14.3 0.0 copy-done.3
  14.3 0.0 copy-done.4
  14.3 1.0 fusion.6
  15.3 0.3 copy.38
  15.7 0.0 copy-start.1
  15.7 0.6 gather_fusion
  16.2 0.0 copy-done
  16.2 0.5 fusion.2
  16.8 0.1 reshape.76.rhs_ref
  16.9 0.0 copy-done.1
  16.9 159.5 %shard_map.73 = f32[1,384]{1,0:T(1,128)S(1)} custom-call(f32[384,384]{1,0:T(8,128)S(1)} %bitcast.40, f32[1,384]{1,0:T(1,128)S(1)} %reshape.76.rhs_ref), custom_call_target="tpu_custom_call" | custom-call | tf_op jit(solution)/shard_map/pallas_call | solution.py:315
  176.4 0.6 copy.48
  (5 shorter events, 0.1 us)
Async XLA Ops:
  0.0 16.2 %copy-start = (f32[1,6,8,256]{3,2,1,0:T(8,128)S(1)}, f32[1,6,8,256]{3,2,1,0:T(8,128)}, u32[]{:S(2)}) copy-start(f32[1,6,8,256]{3,2,1,0:T(8,128)} %param.11) | copy-start | bytes 147460
  1.2 9.1 %copy-start.2 = (f32[1,64,8,256]{3,2,1,0:T(8,128)S(1)}, f32[1,64,8,256]{3,2,1,0:T(8,128)}, u32[]{:S(2)}) copy-start(f32[1,64,8,256]{3,2,1,0:T(8,128)} %param.7) | copy-start | bytes 1572868
  1.4 9.2 %collective-permute-start.2 = (f32[1,64,8,1]{3,1,2,0:T(8,128)S(1)}, f32[1,64,8,1]{3,1,2,0:T(8,128)S(1)}, u32[]{:S(2)}, u32[]{:S(2)}) collective-permute-start(f32[1,64,8,1]{3,1,2,0:T(8,128)S(1)} %get-tuple-element.7), channel_id=1, source_target_pairs={{0,2},{2,4},{4,6},{6,8},{8,10},{10,12},{12,14},{14,0},{1,3},{3,5},... | collective-permute-start | bytes 6152 | tf_op jit(solution)/shard_map/ppermute | solution.py:26
  3.4 10.3 %collective-permute-start.3 = (f32[1,64,8,1]{3,1,2,0:T(8,128)S(1)}, f32[1,64,8,1]{3,1,2,0:T(8,128)S(1)}, u32[]{:S(2)}, u32[]{:S(2)}) collective-permute-start(f32[1,64,8,1]{3,1,2,0:T(8,128)S(1)} %get-tuple-element.8), channel_id=1, source_target_pairs={{2,0},{4,2},{6,4},{8,6},{10,8},{12,10},{14,12},{0,14},{3,1},{5,3},... | collective-permute-start | bytes 6152 | tf_op jit(solution)/shard_map/ppermute | solution.py:27
  6.8 3.5 %copy-start.6 = (s32[1,1,1,6]{3,2,1,0:T(1,128)S(1)}, s32[1,1,1,6]{3,2,1,0:T(1,128)}, u32[]{:S(2)}) copy-start(s32[1,1,1,6]{3,2,1,0:T(1,128)} %param.12) | copy-start | bytes 76
  6.8 3.5 %copy-start.5 = (f32[1,8,256]{2,1,0:T(8,128)S(1)}, f32[1,8,256]{2,1,0:T(8,128)}, u32[]{:S(2)}) copy-start(f32[1,8,256]{2,1,0:T(8,128)} %param.9) | copy-start | bytes 24580
  6.8 6.9 %collective-permute-start = (f32[1,64,1,256]{3,1,2,0:T(8,128)S(1)}, f32[1,64,1,256]{3,1,2,0:T(8,128)S(1)}, u32[]{:S(2)}, u32[]{:S(2)}) collective-permute-start(f32[1,64,1,256]{3,1,2,0:T(8,128)S(1)} %get-tuple-element.5), channel_id=1, source_target_pairs={{16,0},{32,16},{48,32},{64,48},{80,64},{96,80},{112,96},{128,112},... | collective-permute-start | bytes 196616 | tf_op jit(solution)/shard_map/ppermute | solution.py:27
  9.0 5.3 %collective-permute-start.1 = (f32[1,64,1,256]{3,1,2,0:T(8,128)S(1)}, f32[1,64,1,256]{3,1,2,0:T(8,128)S(1)}, u32[]{:S(2)}, u32[]{:S(2)}) collective-permute-start(f32[1,64,1,256]{3,1,2,0:T(8,128)S(1)} %get-tuple-element.6), channel_id=1, source_target_pairs={{0,16},{16,32},{32,48},{48,64},{64,80},{80,96},{96,112},{112,128},... | collective-permute-start | bytes 196616 | tf_op jit(solution)/shard_map/ppermute | solution.py:26
  10.4 4.0 %copy-start.3 = (f32[1,64,8,256]{3,2,1,0:T(8,128)S(1)}, f32[1,64,8,256]{3,2,1,0:T(8,128)}, u32[]{:S(2)}) copy-start(f32[1,64,8,256]{3,2,1,0:T(8,128)} %param.8) | copy-start | bytes 1572868
  10.4 3.9 %copy-start.4 = (f32[1,64,64]{2,1,0:T(8,128)S(1)}, f32[1,64,64]{2,1,0:T(8,128)}, u32[]{:S(2)}) copy-start(f32[1,64,64]{2,1,0:T(8,128)} %param.10) | copy-start | bytes 49156
  15.7 1.2 copy-start.1

commit v2 on v0

v2 whole, which is shorter than its diff:
```python
import functools

import jax
import jax.numpy as jnp
from jax import lax
from jax.experimental import pallas as pl
from jax.experimental.pallas import tpu as pltpu
from jax.sharding import PartitionSpec as P

highest = lax.Precision.HIGHEST
diffusion = 0.5
F32 = jnp.float32
BF16 = jnp.bfloat16
MESH = pl.DeviceIdType.MESH
H = 192
B = 64
W = 256


def mm(a, b):
    return lax.dot_general(a, b, (((1,), (0,)), ((), ())), precision=highest, preferred_element_type=F32)


def mtn(a, b):
    return lax.dot_general(a, b, (((0,), (0,)), ((), ())), precision=highest, preferred_element_type=F32)


def mnt(a, b):
    return lax.dot_general(a, b, (((1,), (1,)), ((), ())), precision=highest, preferred_element_type=F32)


def mnt_narrow(a, b):
    return lax.dot_general(a, b, (((1,), (1,)), ((), ())), preferred_element_type=F32)


def halves(x):
    high = x.astype(BF16)
    return high, (x - high.astype(F32)).astype(BF16)


def row_of(x, i):
    return jnp.broadcast_to(x[i : i + 1, :], x.shape)


def col_of(x, i):
    return jnp.broadcast_to(x[:, i : i + 1], x.shape)


def tree_sum(terms):
    terms = list(terms)
    while len(terms) > 1:
        terms = [terms[i] + terms[i + 1] if i + 1 < len(terms) else terms[i] for i in range(0, len(terms), 2)]
    return terms[0]


def invert8(columns):
    sub = lax.broadcasted_iota(jnp.int32, (8, 128), 0)
    columns = list(columns)
    for p in range(0, 8, 2):
        x, y = columns[p], columns[p + 1]
        a, b, c = row_of(x, p), row_of(y, p), row_of(y, p + 1)
        scale = 1.0 / (a * c - b * b)
        first, second = sub == p, sub == p + 1
        pivot_rows = jnp.logical_or(first, second)
        hu = jnp.where(first, c, jnp.where(second, -b, y * b - x * c))
        hv = jnp.where(first, -b, jnp.where(second, a, x * b - y * a))
        for j in range(8):
            if j in (p, p + 1):
                continue
            u, v = row_of(columns[j], p), row_of(columns[j], p + 1)
            columns[j] = jnp.where(pivot_rows, 0.0, columns[j]) + (hu * u + hv * v) * scale
        columns[p] = hu * scale
        columns[p + 1] = hv * scale
    return columns


def gauss_jordan(tiles, offset):
    count, parts = len(tiles), len(tiles[0])
    sub = lax.broadcasted_iota(jnp.int32, (8, 128), 0)
    lane = lax.broadcasted_iota(jnp.int32, (8, 128), 1)
    for k in range(count):
        start = offset + 8 * k
        block = jnp.logical_and(lane >= start, lane < start + 8)
        inverse = invert8([col_of(tiles[k][0], start + j) for j in range(8)])
        pivot = []
        for l in range(parts):
            value = tiles[k][l]
            if l == 0:
                value = jnp.where(block, jnp.where(lane - start == sub, 1.0, 0.0), value)
            pivot.append(tree_sum([inverse[j] * row_of(value, j) for j in range(8)]))
        rows = [[row_of(pivot[l], j) for j in range(8)] for l in range(parts)]
        for i in [i % count for i in range(k + 1, k + count)]:
            factors = [col_of(tiles[i][0], start + j) for j in range(8)]
            fresh = []
            for l in range(parts):
                base = tiles[i][l]
                if l == 0:
                    base = jnp.where(block, 0.0, base)
                fresh.append(base - tree_sum([factors[j] * rows[l][j] for j in range(8)]))
            tiles[i] = fresh
        tiles[k] = pivot
    return tiles


def packed(m):
    return [
        m[0:B, 0:128],
        jnp.concatenate([m[0:B, 128:H], m[128:H, 128:H]], axis=1),
        jnp.concatenate([m[B:128, 128:H], m[B:128, B:128]], axis=1),
    ]


def tree_kernel(
    sizes, state, source, rate, jac, lift, sep, leaf, out_ref,
    psb, eb, oob, one, two, three, tt, gg, xh, xl, xv, xout, edge_rows, halo_rows, edge_cols, halo_cols,
    up_send, up_recv, halo_send, halo_recv, down_send, down_recv,
):
    n_axial, n_azim, n_bank = sizes
    total = n_axial * n_azim * n_bank
    merges = total.bit_length() - 1
    local = merges - 1
    i_axial, i_azim, i_bank = lax.axis_index("axial"), lax.axis_index("azim"), lax.axis_index("bank")
    me = (i_axial * n_azim + i_azim) * n_bank + i_bank
    channels, rows_here, cells = state.shape

    def device(n):
        return (n // (n_azim * n_bank), (n // n_bank) % n_azim, n % n_bank)

    def field(level):
        bit = level if level < local else merges - 1
        azim_top = (n_bank * n_azim).bit_length() - 2
        if n_azim == 8 and bit == azim_top:
            return bit - 2, 3
        if n_axial == 32 and bit == azim_top + 3:
            return bit - 2, 3
        if n_axial == 32 and bit == azim_top + 5:
            return bit - 1, 2
        return bit, 1

    exchanges = [l for l in range(merges + 1) if l != local]

    def partner_at(level):
        low, width = field(level)
        value = (me // (1 << low)) % (1 << width)
        return me + ((1 << width) - 1 - 2 * value) * (1 << low)

    def partner(level):
        if isinstance(level, int):
            return partner_at(level)
        n = partner_at(0)
        for l in exchanges[1:]:
            n = jnp.where(level == l, partner_at(l), n)
        return n

    def first_slot(level):
        slot = jnp.int32(0)
        for l in range(merges + 1):
            bit = (me // (1 << l)) % 2
            here = 1 if l == local else (0 if l == merges else (1 - bit if l == merges - 2 else bit))
            slot = jnp.where(level == l, here, slot)
        return slot

    def piece(which, level, slot):
        if which == 0:
            return psb.at[level, slot, :, 0:256]
        if which == 1:
            return psb.at[level, slot, :, 256:384]
        return (eb if which == 2 else oob).at[level, slot]

    def upward(level, which):
        return pltpu.make_async_remote_copy(
            src_ref=piece(which, level, 0),
            dst_ref=piece(which, level, 1),
            send_sem=up_send.at[level, which],
            recv_sem=up_recv.at[level, which],
            device_id=device(partner(level)),
            device_id_type=MESH,
        )

    def downward():
        return pltpu.make_async_remote_copy(
            src_ref=xout.at[0],
            dst_ref=xout.at[1],
            send_sem=down_send,
            recv_sem=down_recv,
            device_id=device(partner_at(0)),
            device_id_type=MESH,
        )

    left = (i_axial, lax.rem(i_azim + n_azim - 1, n_azim), i_bank)
    right = (i_axial, lax.rem(i_azim + 1, n_azim), i_bank)
    above = (i_axial - 1, i_azim, i_bank)
    below = (i_axial + 1, i_azim, i_bank)
    has_above, has_below = i_axial > 0, i_axial < n_axial - 1

    def halo(which):
        src, dst, to = (
            (edge_rows.at[0], halo_rows.at[1], above),
            (edge_rows.at[1], halo_rows.at[0], below),
            (edge_cols.at[0], halo_cols.at[1], left),
            (edge_cols.at[1], halo_cols.at[0], right),
        )[which]
        return pltpu.make_async_remote_copy(
            src_ref=src,
            dst_ref=dst,
            send_sem=halo_send.at[which],
            recv_sem=halo_recv.at[which],
            device_id=to,
            device_id_type=MESH,
        )

    halo_rows[...] = jnp.zeros_like(halo_rows)
    barrier = pltpu.get_barrier_semaphore()

    def greet(to):
        pl.semaphore_signal(barrier, inc=1, device_id=to, device_id_type=MESH)

    greet(left)
    greet(right)
    greet(device(partner_at(0)))
    pl.when(has_above)(lambda: greet(above))
    pl.when(has_below)(lambda: greet(below))

    @pl.when(i_bank == 0)
    def _():
        for level in exchanges[1:]:
            greet(device(partner_at(level)))

    lane128 = lax.broadcasted_iota(jnp.int32, (channels, 128), 1)
    edge_rows[0] = state[:, 0, :]
    edge_rows[1] = state[:, rows_here - 1, :]
    first_cols = jnp.zeros((channels, 128), F32)
    last_cols = jnp.zeros((channels, 128), F32)
    for r in range(rows_here):
        head, tail = state[:, r, 0:128], state[:, r, cells - 128 : cells]
        first_cols = jnp.where(lane128 == r, pltpu.roll(head, r, 1) if r else head, first_cols)
        last_cols = jnp.where(lane128 == r, pltpu.roll(tail, r + 1, 1), last_cols)
    edge_cols[0] = first_cols
    edge_cols[1] = last_cols

    def put(ref, level, parts):
        for l in range(3):
            ref[level, 0, :, 128 * l : 128 * l + 128] = parts[l]

    put(psb, 0, packed(leaf[H:, H:]))
    put(oob, 0, packed(leaf[:H, :H]))
    eb[0, 0, :, 0:H] = leaf[H:, :H]
    eb[0, 0, :, H:W] = jnp.zeros((H, W - H), F32)
    psb[local, 1] = jnp.zeros((B, 2 * H), F32)
    oob[local, 1] = jnp.zeros((B, 2 * H), F32)
    eb[local, 1] = jnp.zeros((H, W), F32)
    three[...] = jnp.zeros((B, 2 * B), F32)

    friends = 3 + jnp.where(has_above, 1, 0) + jnp.where(has_below, 1, 0)
    friends = friends + jnp.where(i_bank == 0, len(exchanges) - 1, 0)
    pl.semaphore_wait(barrier, friends)

    @pl.when(i_bank == 1)
    def _():
        for which in (0, 1, 3):
            upward(0, which).start()

    pl.when(has_above)(lambda: halo(0).start())
    pl.when(has_below)(lambda: halo(1).start())
    halo(2).start()
    halo(3).start()

    def front():
        pl.when(has_below)(lambda: halo(0).wait_recv())
        pl.when(has_above)(lambda: halo(1).wait_recv())
        halo(2).wait_recv()
        halo(3).wait_recv()
        lane = lax.broadcasted_iota(jnp.int32, (channels, cells), 1)
        lane6 = lax.broadcasted_iota(jnp.int32, (sep.shape[0], cells), 1)
        jacobian = jac[...]
        rhs = jnp.zeros((channels, sep.shape[0]), F32)
        for r in range(rows_here):
            here = state[:, r, :]
            up = state[:, r - 1, :] if r else halo_rows[0]
            down = state[:, r + 1, :] if r < rows_here - 1 else halo_rows[1]
            before = jnp.where(lane == 0, halo_cols[0][:, r : r + 1], pltpu.roll(here, 1, 1))
            after = jnp.where(lane == cells - 1, halo_cols[1][:, r : r + 1], pltpu.roll(here, cells - 1, 1))
            reaction = mtn(jacobian, rate[r : r + 1, :] * here)
            residual = source[:, r, :] - reaction - diffusion * (4.0 * here - (up + down + before + after))
            picks = jnp.where(lane6 + r * cells == sep[...], 1.0, 0.0)
            rhs = rhs + mnt(residual, picks + lift[:, r, :])
        for c in range(3):
            eb[0, 0, c * channels : (c + 1) * channels, H : H + 1] = rhs[:, c + 3 : c + 4]
            eb[0, 0, c * channels : (c + 1) * channels, H + 1 : H + 2] = rhs[:, c : c + 1]

    @pl.when(i_bank == 1)
    def _():
        front()
        upward(0, 2).start()

    def ascend(level, carry):
        @pl.when(level != local)
        def _():
            upward(level, 0).wait_recv()

        first = first_slot(level)
        second = 1 - first

        def both(i, l):
            rows, lanes = pl.ds(8 * i, 8), pl.ds(128 * l, 128)
            return psb[level, 0, rows, lanes] + psb[level, 1, rows, lanes]

        tiles = gauss_jordan([[both(i, 0), both(i, 1)] for i in range(8)], 0)
        for i in range(8):
            for l in range(2):
                one[8 * i : 8 * i + 8, 128 * l : 128 * l + 128] = tiles[i][l]

        @pl.when(level != local)
        def _():
            upward(level, 1).wait_recv()

        lane = lax.broadcasted_iota(jnp.int32, (B, 128), 1)
        head = psb[level, 0, :, 0:256] + psb[level, 1, :, 0:256]
        k12, k13, k33 = head[:, B:128], head[:, 128:H], head[:, H:]
        update = mtn(k12, one[...])
        two[...] = (
            psb[level, 0, :, 256:384] + psb[level, 1, :, 256:384] - jnp.where(lane < B, update[:, 128:], update[:, :128])
        )
        s23 = two[:, 0:B]
        tiles = gauss_jordan([[two[8 * i : 8 * i + 8, :]] for i in range(8)], B)
        corner = k33 - mtn(k13, one[:, 128:H])
        for i in range(8):
            two[8 * i : 8 * i + 8, :] = tiles[i][0]
        three[:, 0:B] = corner - mtn(s23, two[:, 0:B])

        pl.when(level == 0)(front)

        @pl.when(level != local)
        def _():
            upward(level, 2).wait_recv()

        @pl.when(jnp.logical_and(level != local, level != merges))
        def _():
            upward(level, 3).wait_recv()

        lane = lax.broadcasted_iota(jnp.int32, (H, W), 1)
        e = [eb[level, first], eb[level, second]]
        f = e[0] + e[1]
        outer_f = [e[0][:, 128:W], e[1][:, 128:W]]
        e[0] = jnp.where(lane < H, e[0], jnp.where(lane == H, f, 0.0))
        for q in range(2):
            m1 = mtn(one[:, 0:H], e[q][0:B])
            t2 = e[q][B:128] - m1[B:128]
            m2 = mtn(two[...], t2)
            tt[q, 0:B] = e[q][0:B]
            tt[q, B:128] = t2
            tt[q, 128:H] = e[q][128:H] - m1[128:H] - m2[0:B]
            gg[q, 0:B] = m1[0:B]
            gg[q, B:128] = m2[B:128]
        low = gauss_jordan([[three[8 * i : 8 * i + 8, :]] for i in range(8)], 0)
        before = packed(mtn(tt[1, 0:128, 0:H], gg[1, 0:128, 0:H]))
        for i in range(8):
            three[8 * i : 8 * i + 8, :] = low[i][0]
        gg[1, 128:H] = mm(three[:, 0:B], tt[1, 128:H])
        after = packed(mtn(tt[1, 128:H, 0:H], gg[1, 128:H, 0:H]))
        for l in range(3):
            lanes = pl.ds(128 * l, 128)
            psb[level + 1, 0, :, lanes] = oob[level, second, :, lanes] - before[l] - after[l]

        send = jnp.logical_and(level < merges, level + 1 != local)

        @pl.when(send)
        def _():
            upward(level + 1, 0).start()
            upward(level + 1, 1).start()

        gg[0, 128:H] = mm(three[:, 0:B], tt[0, 128:H])
        lane = lax.broadcasted_iota(jnp.int32, (H, 128), 1)
        cross = mtn(tt[1, :, 0:H], gg[0])
        outer = mtn(tt[0, :, 0:H], gg[0])
        eb[level + 1, 0, :, 0:128] = -cross[:, 0:128]
        shared_f = pltpu.roll(outer_f[1], 127, 1) - cross[:, 128:W]
        outer_f = outer_f[0] - pltpu.roll(outer[:, 128:W], 1, 1)
        eb[level + 1, 0, :, 128:W] = jnp.where(
            lane < B, -cross[:, 128:W], jnp.where(lane == B, shared_f, jnp.where(lane == B + 1, outer_f, 0.0))
        )

        @pl.when(send)
        def _():
            upward(level + 1, 2).start()

        parts = packed(outer)
        for l in range(3):
            lanes = pl.ds(128 * l, 128)
            oob[level + 1, 0, :, lanes] = oob[level, first, :, lanes] - parts[l]

        @pl.when(jnp.logical_and(send, level + 1 != merges))
        def _():
            upward(level + 1, 3).start()

        y12, y13, y23 = one[:, B:128], one[:, 128:H], two[:, 0:B]
        for q in range(2):
            x3 = gg[q, 128:H]
            x2 = gg[q, B:128] - mm(y23, x3)
            x1 = gg[q, 0:B] - mm(y12, x2) - mm(y13, x3)
            for r, x in enumerate((x1, x2, x3)):
                high, low = halves(x)
                xh[level, q, B * r : B * r + B] = high
                xl[level, q, B * r : B * r + B] = low
        return carry

    lane8 = lax.broadcasted_iota(jnp.int32, (8, W), 1)

    def descend(i, carry):
        level = merges - i
        first = first_slot(level)
        y = jnp.zeros((8, H), F32)
        for q in range(2):
            x = jnp.where(lane8 < H, -xv[level + 1, q], jnp.where(lane8 == H, 1.0 - q, 0.0))
            high, low = halves(x)
            y = y + (mnt_narrow(high, xh[level, q]) + (mnt_narrow(low, xh[level, q]) + mnt_narrow(high, xl[level, q])))
        xv[level, 0] = xv[level + 1, first]
        xv[level, 1, :, 0:H] = y
        return carry

    def wait_up(level, carry):
        @pl.when(level != local)
        def _():
            for which in range(3):
                upward(level, which).wait_send()

        @pl.when(jnp.logical_and(level != local, level != merges))
        def _():
            upward(level, 3).wait_send()

        return carry

    @pl.when(i_bank == 0)
    def _():
        lax.fori_loop(0, merges + 1, ascend, 0)
        xv[...] = jnp.zeros_like(xv)
        lax.fori_loop(0, merges + 1, descend, 0)
        xout[0, 0] = xv[1, 1 - first_slot(0)]
        xout[0, 1] = xv[0, 1]
        downward().start()
        out_ref[:, 0:H] = xv[0, 0, 0:1, 0:H]
        out_ref[:, H:] = xv[0, 1, 0:1, 0:H]
        lax.fori_loop(1, merges + 1, wait_up, 0)
        downward().wait_send()

    @pl.when(i_bank == 1)
    def _():
        for which in range(4):
            upward(0, which).wait_send()
        downward().wait_recv()
        out_ref[:, 0:H] = xout[1, 0, 0:1, 0:H]
        out_ref[:, H:] = xout[1, 1, 0:1, 0:H]

    pl.when(has_above)(lambda: halo(0).wait_send())
    pl.when(has_below)(lambda: halo(1).wait_send())
    halo(2).wait_send()
    halo(3).wait_send()


def solve_tree(sizes, state, source, rate, jac, lift, sep, leaf):
    total = sizes[0] * sizes[1] * sizes[2]
    slots = total.bit_length() + 1
    channels, rows, cells = state.shape
    vmem = pl.BlockSpec(memory_space=pltpu.VMEM)
    return pl.pallas_call(
        functools.partial(tree_kernel, sizes),
        out_shape=jax.ShapeDtypeStruct((1, 2 * H), F32),
        in_specs=[vmem] * 7,
        out_specs=vmem,
        scratch_shapes=[
            pltpu.VMEM((slots, 2, B, 2 * H), F32),
            pltpu.VMEM((slots, 2, H, W), F32),
            pltpu.VMEM((slots, 2, B, 2 * H), F32),
            pltpu.VMEM((B, 256), F32),
            pltpu.VMEM((B, 128), F32),
            pltpu.VMEM((B, 128), F32),
            pltpu.VMEM((2, H, W), F32),
            pltpu.VMEM((2, H, W), F32),
            pltpu.VMEM((slots, 2, H, W), BF16),
            pltpu.VMEM((slots, 2, H, W), BF16),
            pltpu.VMEM((slots, 2, 8, W), F32),
            pltpu.VMEM((2, 2, 8, W), F32),
            pltpu.VMEM((2, channels, cells), F32),
            pltpu.VMEM((2, channels, cells), F32),
            pltpu.VMEM((2, channels, 128), F32),
            pltpu.VMEM((2, channels, 128), F32),
            pltpu.SemaphoreType.DMA((slots, 4)),
            pltpu.SemaphoreType.DMA((slots, 4)),
            pltpu.SemaphoreType.DMA((4,)),
            pltpu.SemaphoreType.DMA((4,)),
            pltpu.SemaphoreType.DMA,
            pltpu.SemaphoreType.DMA,
        ],
        compiler_params=pltpu.CompilerParams(
            collective_id=0, has_side_effects=True, vmem_limit_bytes=48 * 1024 * 1024
        ),
    )(state, source, rate, jac, lift, sep, leaf)


def body(sizes, adjoint_state, adjoint_source, reaction_rate, jacobian, lifting, separator, leaf_schur):
    answer = solve_tree(
        sizes,
        adjoint_state[0],
        adjoint_source[0],
        reaction_rate[0],
        jacobian[0],
        lifting[0],
        separator.reshape(-1, 1),
        leaf_schur.reshape(2 * H, 2 * H),
    )
    return answer.reshape(1, 1, 1, 2 * H)


def solution(mesh):
    sizes = (mesh.shape["axial"], mesh.shape["azim"], mesh.shape["bank"])
    in_specs = (
        P("bank", None, "axial", "azim"),
        P("bank", None, "axial", "azim"),
        P("bank", "axial", "azim"),
        P("bank", None, None),
        P("bank", None, "axial", "azim"),
        P("axial", "azim", "bank", None),
        P("axial", "azim", "bank", None, None),
    )
    out_specs = P("axial", "azim", "bank", None)
    return jax.shard_map(
        functools.partial(body, sizes), mesh=mesh, in_specs=in_specs, out_specs=out_specs, check_vma=False
    )
```

time: 918 us -> 141 us (0.15); the launches traced: 903 us -> 140 us
  other arithmetic: 553 us -> 0 us
  Pallas kernels: 0 us -> 134 us
  waiting for transfers between devices: 114 us -> 0 us
  local copies, waits for them, and re-layouts: 80.9 us -> 6.03 us
  starting transfers between devices: 74.3 us -> 0 us
  matrix products: 65.1 us -> 0 us
  between operations: 16.3 us -> 0.02 us
    another operation x134 -> x0, other arithmetic: 535 us -> none  [the longest x63 259 us: eliminate(): factor = jnp.linalg.cholesky(shared_sum)]
    pallas_call x0 -> x1, Pallas kernels: none -> 134 us  [solve_tree(): pl.pallas_call(functools.partial(tree_kernel, sizes), out_shape=jax.Shape...]
    ppermute x22 -> x0, waiting for transfers between devices: 114 us -> none  [the longest x18 111 us: partner(): lax.ppermute(array, axis, [(i, i ^ 1 << distance) for i in range(lax.axis...]
    ppermute x22 -> x0, starting transfers between devices: 74.3 us -> none  [the longest x18 66.5 us: partner(): lax.ppermute(array, axis, [(i, i ^ 1 << distance) for i in range(lax.axis...]
    scatter-add x19 -> x0, local copies, waits for them, and re-layouts: 51.4 us -> none  [the longest x9 28.7 us: body(): parent = parent.at[:middle, :middle].add(first_outer)]
    another operation x140 -> x0, matrix products: 45.5 us -> none  [the longest x27 11.8 us: eliminate(): inner = jax.scipy.linalg.solve_triangular(factor, coupling, lower=True)]
    dot_general x29 -> x0, matrix products: 19.6 us -> none  [the longest x9 8.83 us: body(): parent = -jnp.dot(stacked_cross, coupled, precision=highest)]
    unnamed x156 -> x15, local copies, waits for them, and re-layouts: 17.9 us -> 5.94 us
  transfers between devices with their start and end apart: 22 -> 0, of which waited for: 11 -> 0; matrix products, arithmetic and copies ran while one was open for 4% -> 0% of each run, Pallas kernels for 0% -> 0%
where the time goes in v2:
time: 141 us; the launch traced here: 140 us
  Pallas kernels  134 us (95%)
  local copies, waits for them, and re-layouts  6.03 us (4%)
    pallas_call x1, Pallas kernels, solve_tree(): pl.pallas_call(functools.partial(tree_kernel, sizes), out_shape=jax.Shape...  134 us
    unnamed x15, local copies, waits for them, and re-layouts  5.94 us

profile of v2, /device:TPU:1, one launch (start us, length us, event | category | flops | bytes accessed | tf_op | source)
XLA Modules:
  0.0 140.2 jit_solution(9609481187910007120)
XLA Ops:
  0.0 0.0 copy-start.5
  0.0 0.0 copy-start.6
  0.0 0.7 copy-done.6
  0.7 0.1 copy.8.sep
  0.8 0.0 copy-done.5
  0.8 0.0 copy-start
  0.8 1.1 copy-done
  1.8 0.0 copy-start.1
  1.8 1.0 copy-done.1
  2.9 0.0 copy-start.2
  2.9 1.0 copy-done.2
  3.9 0.0 copy-start.3
  3.9 0.8 copy-done.3
  4.7 0.0 copy-start.4
  4.7 0.8 copy-done.4
  5.5 134.2 %shard_map.73 = f32[1,384]{1,0:T(1,128)S(1)} custom-call(f32[64,8,256]{2,1,0:T(8,128)S(1)} %bitcast.9, f32[64,8,256]{2,1,0:T(8,128)S(1)} %bitcast.10, f32[8,256]{1,0:T(8,128)S(1)} %bitcast.13, f32[64,64]{1,0:T(8,128)S(1)} %bitcast.12, f32[6,8,256]{2,1,0:T(8,128)S(1)} %bitcast.11, s32[6,1]{1,0:T(8,128)S(1)} %copy.8.sep, f32[384,384]{1,0:T(8,128)S(1)} %bitcast.8), custom_call_target="tpu_custom_call" | custom-call | tf_op jit(solution)/shard_map/pallas_call | solution.py:465
  139.6 0.6 copy.10
Async XLA Ops:
  0.0 0.8 copy-start.5
  0.0 0.7 copy-start.6
  0.8 1.1 copy-start
  1.8 1.0 copy-start.1
  2.9 1.0 copy-start.2
  3.9 0.8 copy-start.3
  4.7 0.8 copy-start.4

commit v3 on v2

--- a/solution.py
+++ b/solution.py
@@ -111,7 +111,8 @@
 
 
 def tree_kernel(
-    sizes, state, source, rate, jac, lift, sep, leaf, out_ref,
+    sizes, state_in, source_in, rate_in, jac_in, lift_in, sep, leaf_in, out_ref,
+    state, source, rate, jac, lift, leaf, in_sem,
     psb, eb, oob, one, two, three, tt, gg, xh, xl, xv, xout, edge_rows, halo_rows, edge_cols, halo_cols,
     up_send, up_recv, halo_send, halo_recv, down_send, down_recv,
 ):
@@ -209,6 +210,14 @@
             device_id_type=MESH,
         )
 
+    loads = [
+        pltpu.make_async_copy(src, dst, in_sem.at[i])
+        for i, (src, dst) in enumerate(
+            ((leaf_in, leaf), (state_in, state), (source_in, source), (lift_in, lift), (rate_in, rate), (jac_in, jac))
+        )
+    ]
+    for load in loads:
+        load.start()
     halo_rows[...] = jnp.zeros_like(halo_rows)
     barrier = pltpu.get_barrier_semaphore()
 
@@ -226,6 +235,7 @@
         for level in exchanges[1:]:
             greet(device(partner_at(level)))
 
+    loads[1].wait()
     lane128 = lax.broadcasted_iota(jnp.int32, (channels, 128), 1)
     edge_rows[0] = state[:, 0, :]
     edge_rows[1] = state[:, rows_here - 1, :]
@@ -242,6 +252,7 @@
         for l in range(3):
             ref[level, 0, :, 128 * l : 128 * l + 128] = parts[l]
 
+    loads[0].wait()
     put(psb, 0, packed(leaf[H:, H:]))
     put(oob, 0, packed(leaf[:H, :H]))
     eb[0, 0, :, 0:H] = leaf[H:, :H]
@@ -270,6 +281,8 @@
         pl.when(has_above)(lambda: halo(1).wait_recv())
         halo(2).wait_recv()
         halo(3).wait_recv()
+        for load in loads[2:]:
+            load.wait()
         lane = lax.broadcasted_iota(jnp.int32, (channels, cells), 1)
         lane6 = lax.broadcasted_iota(jnp.int32, (sep.shape[0], cells), 1)
         jacobian = jac[...]
@@ -334,33 +347,33 @@
         def _():
             upward(level, 2).wait_recv()
 
-        @pl.when(jnp.logical_and(level != local, level != merges))
-        def _():
-            upward(level, 3).wait_recv()
-
-        lane = lax.broadcasted_iota(jnp.int32, (H, W), 1)
-        e = [eb[level, first], eb[level, second]]
-        f = e[0] + e[1]
-        outer_f = [e[0][:, 128:W], e[1][:, 128:W]]
-        e[0] = jnp.where(lane < H, e[0], jnp.where(lane == H, f, 0.0))
-        for q in range(2):
-            m1 = mtn(one[:, 0:H], e[q][0:B])
-            t2 = e[q][B:128] - m1[B:128]
-            m2 = mtn(two[...], t2)
-            tt[q, 0:B] = e[q][0:B]
-            tt[q, B:128] = t2
-            tt[q, 128:H] = e[q][128:H] - m1[128:H] - m2[0:B]
-            gg[q, 0:B] = m1[0:B]
-            gg[q, B:128] = m2[B:128]
+        lane = lax.broadcasted_iota(jnp.int32, (H, 128), 1)
+        e_first, e_second = eb[level, first], eb[level, second]
+        tail_first, tail_second = e_first[:, 128:W], e_second[:, 128:W]
+        outer_f = [tail_first, tail_second]
+        tail_first = jnp.where(lane == B, tail_first + tail_second, jnp.where(lane < B, tail_first, 0.0))
+        e = jnp.concatenate([e_second, e_first[:, 0:128], tail_first], axis=1)
+        m1 = mtn(one[:, 0:H], e[0:B])
+        t2 = e[B:128] - m1[B:128]
+        m2 = mtn(two[...], t2)
+        tt[0:B] = e[0:B]
+        tt[B:128] = t2
+        tt[128:H] = e[128:H] - m1[128:H] - m2[0:B]
+        gg[0:B] = m1[0:B]
+        gg[B:128] = m2[B:128]
         low = gauss_jordan([[three[8 * i : 8 * i + 8, :]] for i in range(8)], 0)
-        before = packed(mtn(tt[1, 0:128, 0:H], gg[1, 0:128, 0:H]))
         for i in range(8):
             three[8 * i : 8 * i + 8, :] = low[i][0]
-        gg[1, 128:H] = mm(three[:, 0:B], tt[1, 128:H])
-        after = packed(mtn(tt[1, 128:H, 0:H], gg[1, 128:H, 0:H]))
+
+        @pl.when(jnp.logical_and(level != local, level != merges))
+        def _():
+            upward(level, 3).wait_recv()
+
+        gg[128:H] = mm(three[:, 0:B], tt[128:H])
+        parts = packed(mtn(tt[:, 0:H], gg[:, 0:H]))
         for l in range(3):
             lanes = pl.ds(128 * l, 128)
-            psb[level + 1, 0, :, lanes] = oob[level, second, :, lanes] - before[l] - after[l]
+            psb[level + 1, 0, :, lanes] = oob[level, second, :, lanes] - parts[l]
 
         send = jnp.logical_and(level < merges, level + 1 != local)
 
@@ -369,11 +382,9 @@
             upward(level + 1, 0).start()
             upward(level + 1, 1).start()
 
-        gg[0, 128:H] = mm(three[:, 0:B], tt[0, 128:H])
-        lane = lax.broadcasted_iota(jnp.int32, (H, 128), 1)
-        cross = mtn(tt[1, :, 0:H], gg[0])
-        outer = mtn(tt[0, :, 0:H], gg[0])
+        cross = mtn(tt[:, 0:H], gg[:, W:])
         eb[level + 1, 0, :, 0:128] = -cross[:, 0:128]
+        outer = mtn(tt[:, W : W + H], gg[:, W:])
         shared_f = pltpu.roll(outer_f[1], 127, 1) - cross[:, 128:W]
         outer_f = outer_f[0] - pltpu.roll(outer[:, 128:W], 1, 1)
         eb[level + 1, 0, :, 128:W] = jnp.where(
@@ -393,15 +404,13 @@
         def _():
             upward(level + 1, 3).start()
 
-        y12, y13, y23 = one[:, B:128], one[:, 128:H], two[:, 0:B]
-        for q in range(2):
-            x3 = gg[q, 128:H]
-            x2 = gg[q, B:128] - mm(y23, x3)
-            x1 = gg[q, 0:B] - mm(y12, x2) - mm(y13, x3)
-            for r, x in enumerate((x1, x2, x3)):
-                high, low = halves(x)
-                xh[level, q, B * r : B * r + B] = high
-                xl[level, q, B * r : B * r + B] = low
+        x3 = gg[128:H]
+        x2 = gg[B:128] - mm(two[:, 0:B], x3)
+        x1 = gg[0:B] - mm(one[:, B:128], x2) - mm(one[:, 128:H], x3)
+        for r, x in enumerate((x1, x2, x3)):
+            high, low = halves(x)
+            xh[level, B * r : B * r + B] = high
+            xl[level, B * r : B * r + B] = low
         return carry
 
     lane8 = lax.broadcasted_iota(jnp.int32, (8, W), 1)
@@ -409,11 +418,9 @@
     def descend(i, carry):
         level = merges - i
         first = first_slot(level)
-        y = jnp.zeros((8, H), F32)
-        for q in range(2):
-            x = jnp.where(lane8 < H, -xv[level + 1, q], jnp.where(lane8 == H, 1.0 - q, 0.0))
-            high, low = halves(x)
-            y = y + (mnt_narrow(high, xh[level, q]) + (mnt_narrow(low, xh[level, q]) + mnt_narrow(high, xl[level, q])))
+        x = [jnp.where(lane8 < H, -xv[level + 1, q], jnp.where(lane8 == H, 1.0 - q, 0.0)) for q in (1, 0)]
+        high, low = halves(jnp.concatenate(x, axis=1))
+        y = mnt_narrow(high, xh[level]) + (mnt_narrow(low, xh[level]) + mnt_narrow(high, xl[level]))
         xv[level, 0] = xv[level + 1, first]
         xv[level, 1, :, 0:H] = y
         return carry
@@ -461,23 +468,25 @@
     total = sizes[0] * sizes[1] * sizes[2]
     slots = total.bit_length() + 1
     channels, rows, cells = state.shape
-    vmem = pl.BlockSpec(memory_space=pltpu.VMEM)
+    vmem, hbm = pl.BlockSpec(memory_space=pltpu.VMEM), pl.BlockSpec(memory_space=pl.ANY)
     return pl.pallas_call(
         functools.partial(tree_kernel, sizes),
         out_shape=jax.ShapeDtypeStruct((1, 2 * H), F32),
-        in_specs=[vmem] * 7,
+        in_specs=[hbm] * 5 + [vmem, hbm],
         out_specs=vmem,
         scratch_shapes=[
+            *(pltpu.VMEM(x.shape, F32) for x in (state, source, rate, jac, lift, leaf)),
+            pltpu.SemaphoreType.DMA((6,)),
             pltpu.VMEM((slots, 2, B, 2 * H), F32),
             pltpu.VMEM((slots, 2, H, W), F32),
             pltpu.VMEM((slots, 2, B, 2 * H), F32),
             pltpu.VMEM((B, 256), F32),
             pltpu.VMEM((B, 128), F32),
             pltpu.VMEM((B, 128), F32),
-            pltpu.VMEM((2, H, W), F32),
-            pltpu.VMEM((2, H, W), F32),
-            pltpu.VMEM((slots, 2, H, W), BF16),
-            pltpu.VMEM((slots, 2, H, W), BF16),
+            pltpu.VMEM((H, 2 * W), F32),
+            pltpu.VMEM((H, 2 * W), F32),
+            pltpu.VMEM((slots, H, 2 * W), BF16),
+            pltpu.VMEM((slots, H, 2 * W), BF16),
             pltpu.VMEM((slots, 2, 8, W), F32),
             pltpu.VMEM((2, 2, 8, W), F32),
             pltpu.VMEM((2, channels, cells), F32),

time: 141 us -> 133 us (0.943)
  Pallas kernels: 134 us -> 127 us
    pallas_call x1, Pallas kernels: 134 us -> 127 us  [solve_tree(): pl.pallas_call(functools.partial(tree_kernel, sizes), out_shape=jax.Shape...]
where the time goes in v3:
time: 133 us
  Pallas kernels  127 us (95%)
  local copies, waits for them, and re-layouts  6.03 us (5%)
    pallas_call x1, Pallas kernels, solve_tree(): pl.pallas_call(functools.partial(tree_kernel, sizes), out_shape=jax.Shape...  127 us
    unnamed x15, local copies, waits for them, and re-layouts  5.94 us

profile of v3, /device:TPU:1, one launch (start us, length us, event | category | flops | bytes accessed | tf_op | source)
XLA Modules:
  0.0 133.0 jit_solution(7362667358424687310)
XLA Ops:
  0.0 0.0 copy-start.5
  0.0 0.0 copy-start.6
  0.0 0.7 copy-done.6
  0.7 0.1 copy.8.sep
  0.8 0.0 copy-done.5
  0.8 0.0 copy-start
  0.8 1.1 copy-done
  1.8 0.0 copy-start.1
  1.8 1.0 copy-done.1
  2.9 0.0 copy-start.2
  2.9 1.0 copy-done.2
  3.9 0.0 copy-start.3
  3.9 0.8 copy-done.3
  4.7 0.0 copy-start.4
  4.7 0.8 copy-done.4
  5.5 126.9 %shard_map.73 = f32[1,384]{1,0:T(1,128)S(1)} custom-call(f32[64,8,256]{2,1,0:T(8,128)S(1)} %bitcast.9, f32[64,8,256]{2,1,0:T(8,128)S(1)} %bitcast.10, f32[8,256]{1,0:T(8,128)S(1)} %bitcast.13, f32[64,64]{1,0:T(8,128)S(1)} %bitcast.12, f32[6,8,256]{2,1,0:T(8,128)S(1)} %bitcast.11, s32[6,1]{1,0:T(8,128)S(1)} %copy.8.sep, f32[384,384]{1,0:T(8,128)S(1)} %bitcast.8), custom_call_target="tpu_custom_call" | custom-call | tf_op jit(solution)/shard_map/pallas_call | solution.py:472
  132.4 0.6 copy.10
Async XLA Ops:
  0.0 0.8 copy-start.5
  0.0 0.7 copy-start.6
  0.8 1.1 copy-start
  1.8 1.0 copy-start.1
  2.9 1.0 copy-start.2
  3.9 0.8 copy-start.3
  4.7 0.8 copy-start.4

commit v4 on v3

--- a/solution.py
+++ b/solution.py
@@ -7,7 +7,7 @@
 from jax.experimental.pallas import tpu as pltpu
 from jax.sharding import PartitionSpec as P
 
-highest = lax.Precision.HIGHEST
+highest = lax.Precision.HIGH
 diffusion = 0.5
 F32 = jnp.float32
 BF16 = jnp.bfloat16
@@ -146,8 +146,6 @@
         return me + ((1 << width) - 1 - 2 * value) * (1 << low)
 
     def partner(level):
-        if isinstance(level, int):
-            return partner_at(level)
         n = partner_at(0)
         for l in exchanges[1:]:
             n = jnp.where(level == l, partner_at(l), n)
@@ -168,13 +166,13 @@
             return psb.at[level, slot, :, 256:384]
         return (eb if which == 2 else oob).at[level, slot]
 
-    def upward(level, which):
+    def upward(level, which, to):
         return pltpu.make_async_remote_copy(
             src_ref=piece(which, level, 0),
             dst_ref=piece(which, level, 1),
             send_sem=up_send.at[level, which],
             recv_sem=up_recv.at[level, which],
-            device_id=device(partner(level)),
+            device_id=to,
             device_id_type=MESH,
         )
 
@@ -269,7 +267,7 @@
     @pl.when(i_bank == 1)
     def _():
         for which in (0, 1, 3):
-            upward(0, which).start()
+            upward(0, which, device(partner_at(0))).start()
 
     pl.when(has_above)(lambda: halo(0).start())
     pl.when(has_below)(lambda: halo(1).start())
@@ -304,15 +302,16 @@
     @pl.when(i_bank == 1)
     def _():
         front()
-        upward(0, 2).start()
+        upward(0, 2, device(partner_at(0))).start()
 
     def ascend(level, carry):
-        @pl.when(level != local)
-        def _():
-            upward(level, 0).wait_recv()
-
         first = first_slot(level)
         second = 1 - first
+        above = device(partner(level + 1))
+
+        @pl.when(level != local)
+        def _():
+            upward(level, 0, left).wait_recv()
 
         def both(i, l):
             rows, lanes = pl.ds(8 * i, 8), pl.ds(128 * l, 128)
@@ -325,7 +324,7 @@
 
         @pl.when(level != local)
         def _():
-            upward(level, 1).wait_recv()
+            upward(level, 1, left).wait_recv()
 
         lane = lax.broadcasted_iota(jnp.int32, (B, 128), 1)
         head = psb[level, 0, :, 0:256] + psb[level, 1, :, 0:256]
@@ -345,7 +344,7 @@
 
         @pl.when(level != local)
         def _():
-            upward(level, 2).wait_recv()
+            upward(level, 2, left).wait_recv()
 
         lane = lax.broadcasted_iota(jnp.int32, (H, 128), 1)
         e_first, e_second = eb[level, first], eb[level, second]
@@ -367,7 +366,7 @@
 
         @pl.when(jnp.logical_and(level != local, level != merges))
         def _():
-            upward(level, 3).wait_recv()
+            upward(level, 3, left).wait_recv()
 
         gg[128:H] = mm(three[:, 0:B], tt[128:H])
         parts = packed(mtn(tt[:, 0:H], gg[:, 0:H]))
@@ -379,8 +378,8 @@
 
         @pl.when(send)
         def _():
-            upward(level + 1, 0).start()
-            upward(level + 1, 1).start()
+            upward(level + 1, 0, above).start()
+            upward(level + 1, 1, above).start()
 
         cross = mtn(tt[:, 0:H], gg[:, W:])
         eb[level + 1, 0, :, 0:128] = -cross[:, 0:128]
@@ -393,7 +392,7 @@
 
         @pl.when(send)
         def _():
-            upward(level + 1, 2).start()
+            upward(level + 1, 2, above).start()
 
         parts = packed(outer)
         for l in range(3):
@@ -402,7 +401,7 @@
 
         @pl.when(jnp.logical_and(send, level + 1 != merges))
         def _():
-            upward(level + 1, 3).start()
+            upward(level + 1, 3, above).start()
 
         x3 = gg[128:H]
         x2 = gg[B:128] - mm(two[:, 0:B], x3)
@@ -429,11 +428,11 @@
         @pl.when(level != local)
         def _():
             for which in range(3):
-                upward(level, which).wait_send()
+                upward(level, which, left).wait_send()
 
         @pl.when(jnp.logical_and(level != local, level != merges))
         def _():
-            upward(level, 3).wait_send()
+            upward(level, 3, left).wait_send()
 
         return carry
 
@@ -453,7 +452,7 @@
     @pl.when(i_bank == 1)
     def _():
         for which in range(4):
-            upward(0, which).wait_send()
+            upward(0, which, left).wait_send()
         downward().wait_recv()
         out_ref[:, 0:H] = xout[1, 0, 0:1, 0:H]
         out_ref[:, H:] = xout[1, 1, 0:1, 0:H]
@@ -468,7 +467,7 @@
     total = sizes[0] * sizes[1] * sizes[2]
     slots = total.bit_length() + 1
     channels, rows, cells = state.shape
-    vmem, hbm = pl.BlockSpec(memory_space=pltpu.VMEM), pl.BlockSpec(memory_space=pl.ANY)
+    vmem, hbm = pl.BlockSpec(memory_space=pltpu.VMEM), pl.BlockSpec(memory_space=pltpu.HBM)
     return pl.pallas_call(
         functools.partial(tree_kernel, sizes),
         out_shape=jax.ShapeDtypeStruct((1, 2 * H), F32),
@@ -503,7 +502,7 @@
         compiler_params=pltpu.CompilerParams(
             collective_id=0, has_side_effects=True, vmem_limit_bytes=48 * 1024 * 1024
         ),
-    )(state, source, rate, jac, lift, sep, leaf)
+    )(*(pltpu.with_memory_space_constraint(x, pltpu.HBM) for x in (state, source, rate, jac, lift)), sep, pltpu.with_memory_space_constraint(leaf, pltpu.HBM))
 
 
 def body(sizes, adjoint_state, adjoint_source, reaction_rate, jacobian, lifting, separator, leaf_schur):

time: 133 us -> 120 us (0.902)
  Pallas kernels: 127 us -> 118 us
  local copies, waits for them, and re-layouts: 6.03 us -> 1.31 us
    pallas_call x1, Pallas kernels: 127 us -> 118 us  [solve_tree(): pl.pallas_call(functools.partial(tree_kernel, sizes), out_shape=jax.Shape...]
    unnamed x15 -> x3, local copies, waits for them, and re-layouts: 5.94 us -> 1.22 us
where the time goes in v4:
time: 120 us; the launch traced here: 119 us
  Pallas kernels  118 us (98%)
  local copies, waits for them, and re-layouts  1.31 us (1%)
    pallas_call x1, Pallas kernels, solve_tree(): pl.pallas_call(functools.partial(tree_kernel, sizes), out_shape=jax.Shape...  118 us

profile of v4, /device:TPU:1, one launch (start us, length us, event | category | flops | bytes accessed | tf_op | source)
XLA Modules:
  0.0 119.4 jit_solution(16896939223598419570)
XLA Ops:
  0.0 0.0 copy-start
  0.0 0.7 copy-done
  0.7 0.1 copy.8.sep
  0.7 118.1 %shard_map.73 = f32[1,384]{1,0:T(1,128)S(1)} custom-call(f32[64,8,256]{2,1,0:T(8,128)} %bitcast.10, f32[64,8,256]{2,1,0:T(8,128)} %bitcast.11, f32[8,256]{1,0:T(8,128)} %bitcast.14, f32[64,64]{1,0:T(8,128)} %bitcast.13, f32[6,8,256]{2,1,0:T(8,128)} %bitcast.12, s32[6,1]{1,0:T(8,128)S(1)} %copy.8.sep, f32[384,384]{1,0:T(8,128)} %bitcast.9), custom_call_target="tpu_custom_call" | custom-call | tf_op jit(solution)/shard_map/pallas_call | solution.py:471
  118.8 0.6 copy.10
Async XLA Ops:
  0.0 0.7 copy-start

commit v5 on v4

--- a/solution.py
+++ b/solution.py
@@ -43,7 +43,7 @@
 
 
 def col_of(x, i):
-    return jnp.broadcast_to(x[:, i : i + 1], x.shape)
+    return jnp.take_along_axis(x, jnp.full(x.shape, i, jnp.int32), axis=1, mode="promise_in_bounds")
 
 
 def tree_sum(terms):
@@ -78,27 +78,45 @@
     count, parts = len(tiles), len(tiles[0])
     sub = lax.broadcasted_iota(jnp.int32, (8, 128), 0)
     lane = lax.broadcasted_iota(jnp.int32, (8, 128), 1)
-    for k in range(count):
-        start = offset + 8 * k
-        block = jnp.logical_and(lane >= start, lane < start + 8)
-        inverse = invert8([col_of(tiles[k][0], start + j) for j in range(8)])
-        pivot = []
-        for l in range(parts):
-            value = tiles[k][l]
-            if l == 0:
-                value = jnp.where(block, jnp.where(lane - start == sub, 1.0, 0.0), value)
-            pivot.append(tree_sum([inverse[j] * row_of(value, j) for j in range(8)]))
-        rows = [[row_of(pivot[l], j) for j in range(8)] for l in range(parts)]
-        for i in [i % count for i in range(k + 1, k + count)]:
-            factors = [col_of(tiles[i][0], start + j) for j in range(8)]
+
+    def times(columns, rows):
+        return tree_sum([c * r for c, r in zip(columns, rows)])
+
+    def spread(value):
+        return [row_of(value, j) for j in range(8)]
+
+    def columns_of(value, start):
+        return [col_of(value, start + j) for j in range(8)]
+
+    for p in range(0, count, 2):
+        q = p + 1
+        start = offset + 8 * p
+        block = jnp.logical_and(lane >= start, lane < start + 16)
+        c11, c12 = columns_of(tiles[p][0], start), columns_of(tiles[p][0], start + 8)
+        c21, c22 = columns_of(tiles[q][0], start), columns_of(tiles[q][0], start + 8)
+        i1 = invert8(c11)
+        y = [times(i1, spread(c12[j])) for j in range(8)]
+        corner = [c22[j] - times(c21, spread(y[j])) for j in range(8)]
+        upper, lower = list(tiles[p]), list(tiles[q])
+        upper[0] = jnp.where(block, jnp.where(lane - start == sub, 1.0, 0.0), upper[0])
+        lower[0] = jnp.where(block, jnp.where(lane - start - 8 == sub, 1.0, 0.0), lower[0])
+        upper = [times(i1, spread(t)) for t in upper]
+        lower = [t - times(c21, spread(u)) for t, u in zip(lower, upper)]
+        i2 = invert8(corner)
+        lower = [times(i2, spread(t)) for t in lower]
+        lower_rows = [spread(t) for t in lower]
+        upper = [u - times(y, rows) for u, rows in zip(upper, lower_rows)]
+        upper_rows = [spread(t) for t in upper]
+        for i in [i % count for i in range(q + 1, p + count)]:
+            factors = columns_of(tiles[i][0], start) + columns_of(tiles[i][0], start + 8)
             fresh = []
             for l in range(parts):
                 base = tiles[i][l]
                 if l == 0:
                     base = jnp.where(block, 0.0, base)
-                fresh.append(base - tree_sum([factors[j] * rows[l][j] for j in range(8)]))
+                fresh.append(base - times(factors, upper_rows[l] + lower_rows[l]))
             tiles[i] = fresh
-        tiles[k] = pivot
+        tiles[p], tiles[q] = upper, lower
     return tiles
 
 

time: 120 us -> 109 us (0.908)
  Pallas kernels: 118 us -> 107 us
    pallas_call x1, Pallas kernels: 118 us -> 107 us  [solve_tree(): pl.pallas_call(functools.partial(tree_kernel, sizes), out_shape=jax.Shape...]
where the time goes in v5:
time: 109 us; the launch traced here: 108 us
  Pallas kernels  107 us (98%)
  local copies, waits for them, and re-layouts  1.31 us (1%)
    pallas_call x1, Pallas kernels, solve_tree(): pl.pallas_call(functools.partial(tree_kernel, sizes), out_shape=jax.Shape...  107 us

profile of v5, /device:TPU:1, one launch (start us, length us, event | category | flops | bytes accessed | tf_op | source)
XLA Modules:
  0.0 108.4 jit_solution(1476822279068184802)
XLA Ops:
  0.0 0.0 copy-start
  0.0 0.7 copy-done
  0.7 0.1 copy.8.sep
  0.7 107.1 %shard_map.73 = f32[1,384]{1,0:T(1,128)S(1)} custom-call(f32[64,8,256]{2,1,0:T(8,128)} %bitcast.10, f32[64,8,256]{2,1,0:T(8,128)} %bitcast.11, f32[8,256]{1,0:T(8,128)} %bitcast.14, f32[64,64]{1,0:T(8,128)} %bitcast.13, f32[6,8,256]{2,1,0:T(8,128)} %bitcast.12, s32[6,1]{1,0:T(8,128)S(1)} %copy.8.sep, f32[384,384]{1,0:T(8,128)} %bitcast.9), custom_call_target="tpu_custom_call" | custom-call | tf_op jit(solution)/shard_map/pallas_call | solution.py:489
  107.9 0.6 copy.10
Async XLA Ops:
  0.0 0.7 copy-start

commit v6 on v5

--- a/solution.py
+++ b/solution.py
@@ -179,9 +179,9 @@
 
     def piece(which, level, slot):
         if which == 0:
-            return psb.at[level, slot, :, 0:256]
+            return psb.at[level, slot, :, 0:128]
         if which == 1:
-            return psb.at[level, slot, :, 256:384]
+            return psb.at[level, slot, :, 128:384]
         return (eb if which == 2 else oob).at[level, slot]
 
     def upward(level, which, to):
@@ -331,14 +331,13 @@
         def _():
             upward(level, 0, left).wait_recv()
 
-        def both(i, l):
-            rows, lanes = pl.ds(8 * i, 8), pl.ds(128 * l, 128)
-            return psb[level, 0, rows, lanes] + psb[level, 1, rows, lanes]
-
-        tiles = gauss_jordan([[both(i, 0), both(i, 1)] for i in range(8)], 0)
+        def both(i):
+            rows = pl.ds(8 * i, 8)
+            return psb[level, 0, rows, 0:128] + psb[level, 1, rows, 0:128]
+
+        tiles = gauss_jordan([[both(i)] for i in range(8)], 0)
         for i in range(8):
-            for l in range(2):
-                one[8 * i : 8 * i + 8, 128 * l : 128 * l + 128] = tiles[i][l]
+            one[8 * i : 8 * i + 8, 0:128] = tiles[i][0]
 
         @pl.when(level != local)
         def _():
@@ -346,8 +345,9 @@
 
         lane = lax.broadcasted_iota(jnp.int32, (B, 128), 1)
         head = psb[level, 0, :, 0:256] + psb[level, 1, :, 0:256]
-        k12, k13, k33 = head[:, B:128], head[:, 128:H], head[:, H:]
-        update = mtn(k12, one[...])
+        k13, k33 = head[:, 128:H], head[:, H:]
+        update = mtn(one[:, B:128], head)
+        one[:, 128:H] = mm(one[:, 0:B], k13)
         two[...] = (
             psb[level, 0, :, 256:384] + psb[level, 1, :, 256:384] - jnp.where(lane < B, update[:, 128:], update[:, :128])
         )
@@ -497,7 +497,7 @@
             pltpu.VMEM((slots, 2, B, 2 * H), F32),
             pltpu.VMEM((slots, 2, H, W), F32),
             pltpu.VMEM((slots, 2, B, 2 * H), F32),
-            pltpu.VMEM((B, 256), F32),
+            pltpu.VMEM((B, H), F32),
             pltpu.VMEM((B, 128), F32),
             pltpu.VMEM((B, 128), F32),
             pltpu.VMEM((H, 2 * W), F32),

time: 109 us -> 107 us (0.982)
  Pallas kernels: 107 us -> 105 us
    pallas_call x1, Pallas kernels: 107 us -> 105 us  [solve_tree(): pl.pallas_call(functools.partial(tree_kernel, sizes), out_shape=jax.Shape...]
where the time goes in v6:
time: 107 us
  Pallas kernels  105 us (98%)
  local copies, waits for them, and re-layouts  1.31 us (1%)
    pallas_call x1, Pallas kernels, solve_tree(): pl.pallas_call(functools.partial(tree_kernel, sizes), out_shape=jax.Shape...  105 us

profile of v6, /device:TPU:1, one launch (start us, length us, event | category | flops | bytes accessed | tf_op | source)
XLA Modules:
  0.0 106.5 jit_solution(5296167044965407076)
XLA Ops:
  0.0 0.0 copy-start
  0.0 0.7 copy-done
  0.7 0.1 copy.8.sep
  0.7 105.2 %shard_map.73 = f32[1,384]{1,0:T(1,128)S(1)} custom-call(f32[64,8,256]{2,1,0:T(8,128)} %bitcast.10, f32[64,8,256]{2,1,0:T(8,128)} %bitcast.11, f32[8,256]{1,0:T(8,128)} %bitcast.14, f32[64,64]{1,0:T(8,128)} %bitcast.13, f32[6,8,256]{2,1,0:T(8,128)} %bitcast.12, s32[6,1]{1,0:T(8,128)S(1)} %copy.8.sep, f32[384,384]{1,0:T(8,128)} %bitcast.9), custom_call_target="tpu_custom_call" | custom-call | tf_op jit(solution)/shard_map/pallas_call | solution.py:489
  106.0 0.6 copy.10
Async XLA Ops:
  0.0 0.7 copy-start

commit v7 on v6

--- a/solution.py
+++ b/solution.py
@@ -382,44 +382,47 @@
         for i in range(8):
             three[8 * i : 8 * i + 8, :] = low[i][0]
 
-        @pl.when(jnp.logical_and(level != local, level != merges))
+        gg[128:H] = mm(three[:, 0:B], tt[128:H])
+
+        @pl.when(level < merges)
         def _():
-            upward(level, 3, left).wait_recv()
-
-        gg[128:H] = mm(three[:, 0:B], tt[128:H])
-        parts = packed(mtn(tt[:, 0:H], gg[:, 0:H]))
-        for l in range(3):
-            lanes = pl.ds(128 * l, 128)
-            psb[level + 1, 0, :, lanes] = oob[level, second, :, lanes] - parts[l]
-
-        send = jnp.logical_and(level < merges, level + 1 != local)
-
-        @pl.when(send)
-        def _():
-            upward(level + 1, 0, above).start()
-            upward(level + 1, 1, above).start()
-
-        cross = mtn(tt[:, 0:H], gg[:, W:])
-        eb[level + 1, 0, :, 0:128] = -cross[:, 0:128]
-        outer = mtn(tt[:, W : W + H], gg[:, W:])
-        shared_f = pltpu.roll(outer_f[1], 127, 1) - cross[:, 128:W]
-        outer_f = outer_f[0] - pltpu.roll(outer[:, 128:W], 1, 1)
-        eb[level + 1, 0, :, 128:W] = jnp.where(
-            lane < B, -cross[:, 128:W], jnp.where(lane == B, shared_f, jnp.where(lane == B + 1, outer_f, 0.0))
-        )
-
-        @pl.when(send)
-        def _():
-            upward(level + 1, 2, above).start()
-
-        parts = packed(outer)
-        for l in range(3):
-            lanes = pl.ds(128 * l, 128)
-            oob[level + 1, 0, :, lanes] = oob[level, first, :, lanes] - parts[l]
-
-        @pl.when(jnp.logical_and(send, level + 1 != merges))
-        def _():
-            upward(level + 1, 3, above).start()
+            @pl.when(level != local)
+            def _():
+                upward(level, 3, left).wait_recv()
+
+            parts = packed(mtn(tt[:, 0:H], gg[:, 0:H]))
+            for l in range(3):
+                lanes = pl.ds(128 * l, 128)
+                psb[level + 1, 0, :, lanes] = oob[level, second, :, lanes] - parts[l]
+
+            send = jnp.logical_and(level < merges, level + 1 != local)
+
+            @pl.when(send)
+            def _():
+                upward(level + 1, 0, above).start()
+                upward(level + 1, 1, above).start()
+
+            cross = mtn(tt[:, 0:H], gg[:, W:])
+            eb[level + 1, 0, :, 0:128] = -cross[:, 0:128]
+            outer = mtn(tt[:, W : W + H], gg[:, W:])
+            shared_f = pltpu.roll(outer_f[1], 127, 1) - cross[:, 128:W]
+            own_f = outer_f[0] - pltpu.roll(outer[:, 128:W], 1, 1)
+            eb[level + 1, 0, :, 128:W] = jnp.where(
+                lane < B, -cross[:, 128:W], jnp.where(lane == B, shared_f, jnp.where(lane == B + 1, own_f, 0.0))
+            )
+
+            @pl.when(send)
+            def _():
+                upward(level + 1, 2, above).start()
+
+            parts = packed(outer)
+            for l in range(3):
+                lanes = pl.ds(128 * l, 128)
+                oob[level + 1, 0, :, lanes] = oob[level, first, :, lanes] - parts[l]
+
+            @pl.when(jnp.logical_and(send, level + 1 != merges))
+            def _():
+                upward(level + 1, 3, above).start()
 
         x3 = gg[128:H]
         x2 = gg[B:128] - mm(two[:, 0:B], x3)

time: 107 us -> 107 us (level)
  no operation moved by 1% of the time
where the time goes in v7:
time: 107 us
  Pallas kernels  106 us (99%)
  local copies, waits for them, and re-layouts  1.31 us (1%)
    pallas_call x1, Pallas kernels, solve_tree(): pl.pallas_call(functools.partial(tree_kernel, sizes), out_shape=jax.Shape...  106 us

profile of v7, /device:TPU:1, one launch (start us, length us, event | category | flops | bytes accessed | tf_op | source)
XLA Modules:
  0.0 107.0 jit_solution(7569205839743246137)
XLA Ops:
  0.0 0.0 copy-start
  0.0 0.7 copy-done
  0.7 0.1 copy.8.sep
  0.7 105.7 %shard_map.73 = f32[1,384]{1,0:T(1,128)S(1)} custom-call(f32[64,8,256]{2,1,0:T(8,128)} %bitcast.10, f32[64,8,256]{2,1,0:T(8,128)} %bitcast.11, f32[8,256]{1,0:T(8,128)} %bitcast.14, f32[64,64]{1,0:T(8,128)} %bitcast.13, f32[6,8,256]{2,1,0:T(8,128)} %bitcast.12, s32[6,1]{1,0:T(8,128)S(1)} %copy.8.sep, f32[384,384]{1,0:T(8,128)} %bitcast.9), custom_call_target="tpu_custom_call" | custom-call | tf_op jit(solution)/shard_map/pallas_call | solution.py:492
  106.4 0.6 copy.10
Async XLA Ops:
  0.0 0.7 copy-start
